TPU v7x, 512 devices: a whole 4x8x8 slice. The times are simulated.
512 devices in a mesh: rows: 32 (over z, x), seq: 16 (over y, core).
Axes of the slice: x: 4, y: 8, z: 8, core: 2. Of those that a mesh axis runs over, the one named last changes fastest.
Arguments:
- qkv: bfloat16 [32, 1024, 3840], P('rows', 'seq'), may hold values from -24 to 24
- hidden: bfloat16 [32, 1024, 1280], P('rows', 'seq'), may hold values from -3 to 3
- segment_ids: int32 [32, 1024], P('rows', 'seq'), may hold values from 0 to 4, as said below
- key_keep: int32 [32, 1024], P('rows', 'seq'), may hold values 0 or 1
- grid_sizes: int32 [32, 4, 2], P('rows'), may hold values from 8 to 16, as said below
- owner_slots: int32 [32, 4], P('rows'), may hold values from 0 to 15, as said below
- out_weight: bfloat16 [1280, 1280], P('rows'), may hold values from -0.15625 to 0.15625
- norm_gain: float32 [1280], replicated, may hold values from 0.5 to 1.5
- norm_bias: float32 [1280], replicated, may hold values from -1.5 to 1.5
- merge_weight: bfloat16 [5120, 4096], P(None, 'seq'), may hold values from -0.078125 to 0.078125
Outputs:
- normed: bfloat16 [32, 1024, 1280], P('rows', 'seq')
- request_norm: float32 [32, 16], P('rows', 'seq')
- request_peak: float32 [32, 16], P('rows', 'seq')
Inputs may be any that keep to these rules, and one draw needn't show every extreme that they name: `segment_ids`: segment ids never fall along a pack: image j covers h_j w_j tokens right after image j - 1, and tokens after the last image carry 4; every pack ends with some such padding. Inside an image each aligned group of 4 tokens is one 2 x 2 block of the patch grid, blocks in row-major order. `grid_sizes`: both sides are even; rows run from 8 to 16, columns from 8 to 14; the first image of every pack has 16 rows and 14 columns; the images of a pack agree with segment_ids. `owner_slots`: the images of one pack have distinct slots.
All inputs are finite; a program needn't handle non-finite values. No bound on the sum of `key_keep` on one device may be relied on, other than what follows from the above.
Results may differ from a plain program's by a relative error of at most 0.0057.
Values may be sent and summed in bfloat16 or wider, within the bound.
No kernel may reach another device: no remote copies, remote signals or barrier semaphores. Data moves between devices by JAX's collectives and lax.ppermute only.
A program may use at most 64 MiB of HBM per device.

v0:
```python
import jax
import jax.numpy as jnp
import numpy as np
from jax import lax
from jax.experimental import pallas as pl
from jax.experimental.pallas import tpu as pltpu
from jax.sharding import PartitionSpec as P


D = 1280
HEADS = 16
HD = 80
OUT = 4096
IMGS = 4
SEQ = 1024
TOK = 64
CHIPS = 8
MAXIMG = 896
NEG = -1e30


F32 = jnp.float32
BF16 = jnp.bfloat16
VM = pl.BlockSpec(memory_space=pltpu.VMEM)
SM = pl.BlockSpec(memory_space=pltpu.SMEM)


def iota(shape, dim):
    return lax.broadcasted_iota(jnp.int32, shape, dim)


def image_bounds(grid_ref):
    starts, ends, total = [], [], 0
    for j in range(IMGS):
        starts.append(total)
        total = total + grid_ref[0, j, 0] * grid_ref[0, j, 1]
        ends.append(total)
    return starts, ends


def rotary_kernel(grid_ref, keep_ref, qkv_ref, out_ref):
    starts, ends = image_bounds(grid_ref)
    place = lax.axis_index("seq") * TOK + iota((TOK, 256), 0)
    begin = jnp.zeros((TOK, 256), jnp.int32)
    width = jnp.full((TOK, 256), 2, jnp.int32)
    for j in range(IMGS):
        inside = (place >= starts[j]) & (place < ends[j])
        begin = jnp.where(inside, starts[j], begin)
        width = jnp.where(inside, grid_ref[0, j, 1], width)
    valid = place < ends[IMGS - 1]
    offset = place - begin
    square = lax.shift_right_logical(offset, 2)
    corner = offset & 3
    half = lax.shift_right_logical(width, 1)
    line = jnp.floor((square.astype(F32) + 0.5) / half.astype(F32)).astype(jnp.int32)
    row = 2 * line + lax.shift_right_logical(corner, 1)
    col = 2 * (square - line * half) + (corner & 1)
    row = jnp.where(valid, row, 0).astype(F32)
    col = jnp.where(valid, col, 0).astype(F32)
    lane = iota((TOK, 256), 1) & 127
    rotated = lane < HD
    pair = lane
    for _ in range(5):
        pair = jnp.where(pair >= 20, pair - 20, pair)
    rate = jnp.exp(pair.astype(F32) * (-np.log(10000.0) / 20))
    angle = jnp.where(lane < HD // 2, row, col) * rate
    cosine = jnp.where(rotated, jnp.cos(angle), 1.0)
    low = (lane < 20) | ((lane >= 40) & (lane < 60))
    sine = jnp.sin(angle)
    sine = jnp.where(rotated, jnp.where(low, -sine, sine), 0.0)
    diagonal = iota((TOK, TOK), 0) == iota((TOK, TOK), 1)
    flags = jnp.where(diagonal, keep_ref[...].astype(F32), 0.0)
    tail = jnp.broadcast_to(jnp.sum(flags, axis=1, keepdims=True), (TOK, 16))
    for dest in range(HEADS):
        q = qkv_ref[0, :, dest * HD : dest * HD + HD].astype(F32)
        k = qkv_ref[0, :, D + dest * HD : D + dest * HD + HD].astype(F32)
        v = qkv_ref[0, :, 2 * D + dest * HD : 2 * D + dest * HD + HD].astype(F32)
        full = jnp.concatenate([q, v[:, :48], k, v[:, 48:], tail], axis=1)
        swapped = jnp.where(low, pltpu.roll(full, 256 - 20, 1), pltpu.roll(full, 20, 1))
        out_ref[dest] = (full * cosine + swapped * sine).astype(BF16)


def attention_kernel(grid_ref, x_ref, out_ref):
    starts, ends = image_bounds(grid_ref)
    pick = jnp.where(iota((8, 128), 1) == 112, 1.0, 0.0).astype(BF16)
    keep = lax.dot_general(
        pick, x_ref[:, 128:], (((1,), (1,)), ((), ())), preferred_element_type=F32
    )[0:1]
    key_place = jnp.where(keep > 0.5, iota((1, SEQ), 1), -1)
    query_lane = iota((128, 128), 1) < HD

    def emit(chip, rows):
        flipped = jnp.transpose(rows)
        out_ref[chip] = jnp.concatenate(
            [flipped[80:128], flipped[208:240]], axis=0
        ).astype(BF16)

    for chip in range(MAXIMG // 128):
        first = chip * 128
        low = max(0, first - 256)
        high = min(MAXIMG, first + 384)
        query = jnp.where(query_lane, x_ref[first : first + 128, 0:128], 0)
        scores = lax.dot_general(
            query,
            x_ref[low:high, 128:256],
            (((1,), (1,)), ((), ())),
            preferred_element_type=F32,
        ) * HD ** (-0.5)
        place = first + iota((128, 1), 0)
        lo = place
        hi = place
        for j in range(IMGS):
            inside = (place >= starts[j]) & (place < ends[j])
            lo = jnp.where(inside, starts[j], lo)
            hi = jnp.where(inside, ends[j], hi)
        keys = key_place[:, low:high]
        same = (keys >= lo) & (keys < hi)
        own = iota((1, high - low), 1) + low == place
        scores = jnp.where(same | own, scores, NEG)
        top = jnp.max(scores, axis=1, keepdims=True)
        weights = jnp.exp(scores - top)
        total = jnp.sum(weights, axis=1, keepdims=True)
        summed = jnp.dot(
            weights.astype(BF16), x_ref[low:high, :], preferred_element_type=F32
        )
        emit(chip, summed / total)
    emit(CHIPS - 1, x_ref[MAXIMG:SEQ, :].astype(F32))


def mix_kernel(heads_ref, weight_ref, hidden_ref, own_ref, send_ref, part_ref):
    part_ref[...] = lax.dot_general(
        heads_ref[...],
        weight_ref[...],
        (((0,), (0,)), ((), ())),
        preferred_element_type=F32,
    )
    core = lax.axis_index("seq") & 1
    mine = pl.multiple_of(core * TOK, TOK)
    other = pl.multiple_of((1 - core) * TOK, TOK)
    own_ref[...] = part_ref[pl.ds(mine, TOK), :] + hidden_ref[0].astype(F32)
    send_ref[...] = part_ref[pl.ds(other, TOK), :]


def norm_kernel(own_ref, recv_ref, gain_ref, bias_ref, normed_ref, block_ref):
    mixed = own_ref[...] + recv_ref[...]
    centred = mixed - jnp.mean(mixed, axis=1, keepdims=True)
    spread = jnp.mean(centred * centred, axis=1, keepdims=True)
    normed = centred * lax.rsqrt(spread + 1e-05) * gain_ref[...].reshape(1, D) + bias_ref[...].reshape(1, D)
    normed = normed.astype(BF16)
    normed_ref[0] = normed
    line = iota((TOK, TOK), 0)
    source = 4 * (line & 15) + lax.shift_right_logical(line, 4)
    order = jnp.where(iota((TOK, TOK), 1) == source, 1.0, 0.0).astype(BF16)
    block = jnp.dot(order, normed, preferred_element_type=F32).astype(BF16)
    for chip in range(CHIPS):
        block_ref[chip] = block


def project_kernel(grid_ref, owner_ref, wa_ref, wb_ref, blocks_ref, out_ref):
    halves = []
    for w_ref in (wa_ref, wb_ref):
        part = 0.0
        for corner in range(4):
            rows = jnp.concatenate(
                [blocks_ref[c, 16 * corner : 16 * corner + 16, :] for c in range(CHIPS)],
                axis=0,
            )
            part = part + jnp.dot(
                rows, w_ref[D * corner : D * corner + D, :], preferred_element_type=F32
            )
        halves.append(part)
    done = jnp.concatenate(halves, axis=1)
    squares = jnp.sum(done * done, axis=1, keepdims=True)
    peaks = jnp.max(done, axis=1, keepdims=True)
    _, ends = image_bounds(grid_ref)
    line = iota((128, 128), 0)
    source = 2 * lax.shift_right_logical(line, 4) + (lax.axis_index("seq") & 1)
    token = source * TOK + 4 * (line & 15)
    slot = jnp.full((128, 128), -1, jnp.int32)
    for j in reversed(range(IMGS)):
        slot = jnp.where(token < ends[j], owner_ref[0, j], slot)
    hot = slot == iota((128, 128), 1)
    sums = jnp.sum(jnp.where(hot, squares, 0.0), axis=0, keepdims=True)
    tops = jnp.max(jnp.where(hot, peaks, NEG), axis=0, keepdims=True)
    both = jnp.where(line == 0, sums, jnp.where(line == 1, tops, 0.0))
    out_ref[...] = jnp.transpose(both)[:16]


def final_kernel(grid_ref, owner_ref, stats_ref, norm_ref, peak_ref):
    stats = stats_ref[...]
    total = jnp.sum(stats, axis=0, keepdims=True)[:, 0:1]
    top = jnp.max(stats, axis=0, keepdims=True)[:, 1:2]
    me = lax.axis_index("seq")
    count = 0
    for j in range(IMGS):
        size = lax.shift_right_logical(grid_ref[0, j, 0] * grid_ref[0, j, 1], 2)
        count = count + jnp.where(owner_ref[0, j] == me, size, 0)
    counts = jnp.full((1, 1), count, jnp.int32)
    divisor = (jnp.maximum(counts, 1) * OUT).astype(F32)
    norm_ref[...] = jnp.where(counts > 0, jnp.sqrt(total / divisor + 1e-06), 0.0)
    peak_ref[...] = jnp.where(counts > 0, top, 0.0)


def call(kernel, out, specs, scratch=(), flops=0, bytes_accessed=0, mib=8):
    many = isinstance(out, (tuple, list))
    return pl.pallas_call(
        kernel,
        out_shape=out,
        in_specs=specs,
        out_specs=tuple([VM] * len(out)) if many else VM,
        scratch_shapes=scratch,
        cost_estimate=pl.CostEstimate(
            flops=flops, bytes_accessed=bytes_accessed, transcendentals=0
        ),
        compiler_params=pltpu.CompilerParams(vmem_limit_bytes=mib << 20),
    )


def shape(dims, dtype):
    return jax.ShapeDtypeStruct(dims, dtype)


def chip_shift(x, step, flip=0):
    pairs = []
    for s in range(2 * CHIPS):
        chip, core = s // 2, s % 2
        pairs.append((s, ((chip + step) % CHIPS) * 2 + (core ^ flip)))
    return lax.ppermute(x, "seq", pairs)


def gather_weight(weight):
    groups = [[z * 4 + x for z in range(8)] for x in range(4)]
    column = lax.all_to_all(
        jnp.broadcast_to(weight[None], (8, 40, D)),
        "rows",
        split_axis=0,
        concat_axis=0,
        axis_index_groups=groups,
        tiled=True,
    )

    def shift_x(step, cores):
        pairs = []
        for r in range(32):
            z, x = r // 4, r % 4
            for s in range(16):
                if (x - 2 * (s % 2)) % 4 in cores:
                    pairs.append((r * 16 + s, (z * 4 + (x + step) % 4) * 16 + s))
        return lax.ppermute(column, ("rows", "seq"), pairs)

    two = shift_x(2, (0, 1))
    plus = shift_x(1, (0, 1))
    minus = shift_x(-1, (0, 1))
    rel = (lax.axis_index("rows") - 2 * (lax.axis_index("seq") % 2)) % 4

    def pick(a, b, c, d):
        return jnp.where(
            rel == 0, a, jnp.where(rel == 1, b, jnp.where(rel == 2, c, d))
        )

    pair = jnp.concatenate(
        [pick(column, plus, two, minus), pick(minus, column, plus, two)], axis=1
    )
    return pair.reshape(640, D)


def body(
    qkv,
    hidden,
    segment_ids,
    key_keep,
    grid_sizes,
    owner_slots,
    out_weight,
    norm_gain,
    norm_bias,
    merge_weight,
):
    del segment_ids
    weight = gather_weight(out_weight)
    packed = call(
        rotary_kernel,
        shape((HEADS, TOK, 256), BF16),
        [SM, VM, VM],
        flops=1 << 22,
        bytes_accessed=1 << 20,
    )(grid_sizes, key_keep, qkv)
    heads_all = lax.all_to_all(packed, "seq", split_axis=0, concat_axis=0, tiled=True)
    merge_other = chip_shift(merge_weight, 0, 1)
    head_out = call(
        attention_kernel,
        shape((CHIPS, HD, 128), BF16),
        [SM, VM],
        flops=1 << 29,
        bytes_accessed=1 << 20,
    )(grid_sizes, heads_all.reshape(SEQ, 256))
    groups = [[2 * c + p for c in range(CHIPS)] for p in range(2)]
    attended = lax.all_to_all(
        head_out,
        "seq",
        split_axis=0,
        concat_axis=0,
        axis_index_groups=groups,
        tiled=True,
    ).reshape(640, 128)
    own, send = call(
        mix_kernel,
        (shape((TOK, D), F32), shape((TOK, D), F32)),
        [VM, VM, VM],
        scratch=[pltpu.VMEM((128, D), F32)],
        flops=1 << 28,
        bytes_accessed=3 << 20,
    )(attended, weight, hidden)
    recv = chip_shift(send, 0, 1)
    normed, blocks = call(
        norm_kernel,
        (shape((1, TOK, D), BF16), shape((CHIPS, TOK, D), BF16)),
        [VM] * 4,
        flops=1 << 22,
        bytes_accessed=1 << 20,
    )(own, recv, norm_gain, norm_bias)
    blocks = lax.all_to_all(
        blocks,
        "seq",
        split_axis=0,
        concat_axis=0,
        axis_index_groups=groups,
        tiled=True,
    )
    stats = call(
        project_kernel,
        shape((16, 128), F32),
        [SM, SM, VM, VM, VM],
        flops=1 << 29,
        bytes_accessed=7 << 20,
        mib=16,
    )(grid_sizes, owner_slots, merge_weight, merge_other, blocks)
    stats = lax.all_to_all(stats, "seq", split_axis=0, concat_axis=0, tiled=True)
    norm, peak = call(
        final_kernel, (shape((1, 1), F32), shape((1, 1), F32)), [SM, SM, VM]
    )(grid_sizes, owner_slots, stats)
    return (normed, norm, peak)


def solution(mesh):
    placed = (
        P("rows", "seq", None),
        P("rows", "seq", None),
        P("rows", "seq"),
        P("rows", "seq"),
        P("rows", None, None),
        P("rows", None),
        P("rows", None),
        P(),
        P(),
        P(None, "seq"),
    )

    return jax.shard_map(
        body,
        mesh=mesh,
        in_specs=placed,
        out_specs=(P("rows", "seq", None), P("rows", "seq"), P("rows", "seq")),
        check_vma=False,
    )
```

profile of v0, /device:TPU:1, one launch (start us, length us, event | category | flops | bytes accessed | tf_op | source)
XLA Modules:
  0.0 139.5 jit_solution(3992172560717694189)
XLA Ops:
  0.7 1.9 %broadcast_in_dim.2 = bf16[8,40,1280]{2,1,0:T(8,128)(2,1)} broadcast(bf16[40,1280]{1,0:T(8,128)(2,1)} %param.15), dimensions={1,2} | broadcast | bytes 921600 | tf_op jit(solution)/shard_map/broadcast_in_dim | solution.py:234
  2.6 10.9 %all-to-all-start.2 = ((bf16[8,40,1280]{2,1,0:T(8,128)(2,1)}), bf16[8,40,1280]{2,1,0:T(8,128)(2,1)S(1)}, u32[]{:S(2)}, u32[]{:S(2)}) async-start(bf16[8,40,1280]{2,1,0:T(8,128)(2,1)} %broadcast_in_dim.2), calls=%async_computation.2 | async-start | bytes 1638400 | tf_op jit(solution)/shard_map/all_to_all | solution.py:233
  13.5 3.3 %shard_map.112 = bf16[16,64,256]{2,1,0:T(8,128)(2,1)} custom-call(s32[1,4,2]{2,1,0:T(4,128)S(1)} %copy.17.grid_ref, s32[1,64]{1,0:T(1,128)S(1)} %copy-done.6, bf16[1,64,3840]{2,1,0:T(8,128)(2,1)S(1)} %copy-done.1), custom_call_target="tpu_custom_call" | custom-call | flops 4194304 | bytes 1048576 | tf_op jit(solution)/shard_map/pallas_call | solution.py:281
  16.8 20.9 %all-to-all-done.2 = bf16[8,40,1280]{2,1,0:T(8,128)(2,1)S(1)} async-done(((bf16[8,40,1280]{2,1,0:T(8,128)(2,1)}), bf16[8,40,1280]{2,1,0:T(8,128)(2,1)S(1)}, u32[]{:S(2)}, u32[]{:S(2)}) %all-to-all-start.2) | async-done | bytes 819232 | tf_op jit(solution)/shard_map/all_to_all | solution.py:233
  37.7 7.6 %all-to-all-start = ((bf16[16,64,256]{2,1,0:T(8,128)(2,1)}), bf16[16,64,256]{2,1,0:T(8,128)(2,1)S(1)}, u32[]{:S(2)}, u32[]{:S(2)}) async-start(bf16[16,64,256]{2,1,0:T(8,128)(2,1)} %shard_map.112), calls=%async_computation | async-start | bytes 1048576 | tf_op jit(solution)/shard_map/all_to_all | solution.py:288
  45.3 1.3 collective-permute-start
  46.6 1.3 collective-permute-start.1
  47.9 1.6 %collective-permute-start.2 = (bf16[8,40,1280]{2,1,0:T(8,128)(2,1)S(1)}, bf16[8,40,1280]{2,1,0:T(8,128)(2,1)}, u32[]{:S(2)}, u32[]{:S(2)}) collective-permute-start(bf16[8,40,1280]{2,1,0:T(8,128)(2,1)S(1)} %all-to-all-done.2), channel_id=1, source_target_pairs={{0,48},{2,50},{4,52},{6,54},{8,56},{10,58},{12,60},{14,62},{16,0},... | collective-permute-start | bytes 2457608 | tf_op jit(solution)/shard_map/ppermute | solution.py:249
  49.5 13.0 %all-to-all-done = bf16[16,64,256]{2,1,0:T(8,128)(2,1)S(1)} async-done(((bf16[16,64,256]{2,1,0:T(8,128)(2,1)}), bf16[16,64,256]{2,1,0:T(8,128)(2,1)S(1)}, u32[]{:S(2)}, u32[]{:S(2)}) %all-to-all-start) | async-done | bytes 524320 | tf_op jit(solution)/shard_map/all_to_all | solution.py:288
  62.5 3.0 %shard_map.113 = bf16[8,80,128]{2,1,0:T(8,128)(2,1)} custom-call(s32[1,4,2]{2,1,0:T(4,128)S(1)} %copy.17.grid_ref, bf16[1024,256]{1,0:T(8,128)(2,1)S(1)} %bitcast.9), custom_call_target="tpu_custom_call" | custom-call | flops 536870912 | bytes 1048576 | tf_op jit(solution)/shard_map/pallas_call | solution.py:290
  65.5 3.4 %all-to-all-start.1 = ((bf16[8,80,128]{2,1,0:T(8,128)(2,1)}), bf16[8,80,128]{2,1,0:T(8,128)(2,1)S(1)}, u32[]{:S(2)}, u32[]{:S(2)}) async-start(bf16[8,80,128]{2,1,0:T(8,128)(2,1)} %shard_map.113), calls=%async_computation.1 | async-start | bytes 327680 | tf_op jit(solution)/shard_map/all_to_all | solution.py:298
  68.9 0.5 collective-permute-done.1
  69.5 1.6 %select_select_fusion.1 = (bf16[8,40,1280]{2,1,0:T(8,128)(2,1)S(1)}, bf16[8,40,1280]{2,1,0:T(8,128)(2,1)S(1)}) fusion(bf16[8,40,1280]{2,1,0:T(8,128)(2,1)S(1)} %all-to-all-done.2, bf16[8,40,1280]{2,1,0:T(8,128)(2,1)S(1)} %collective-permute-done, bf16[8,40,1280]{2,1,0:T(8,128)(2,1)} %collective-permute-done.1, ...), kind=kLoop, calls=%fused_computation.2 | loop fusion | flops 2457600 | bytes 4915203 | tf_op jit(solution)/shard_map/jit(_where)/select_n | solution.py:257
  71.3 7.9 %all-to-all-done.1 = bf16[8,80,128]{2,1,0:T(8,128)(2,1)S(1)} async-done(((bf16[8,80,128]{2,1,0:T(8,128)(2,1)}), bf16[8,80,128]{2,1,0:T(8,128)(2,1)S(1)}, u32[]{:S(2)}, u32[]{:S(2)}) %all-to-all-start.1) | async-done | bytes 163872 | tf_op jit(solution)/shard_map/all_to_all | solution.py:298
  79.1 0.5 shard_map.114
  79.7 2.3 %collective-permute-start.3 = (f32[64,1280]{1,0:T(8,128)S(1)}, f32[64,1280]{1,0:T(8,128)S(1)}, u32[]{:S(2)}, u32[]{:S(2)}) collective-permute-start(f32[64,1280]{1,0:T(8,128)S(1)} %get-tuple-element.10), channel_id=1, source_target_pairs={{0,1},{1,0},{2,3},{3,2},{4,5},{5,4},{6,7},{7,6},{8,9},{9,8},{10,11... | collective-permute-start | bytes 983048 | tf_op jit(solution)/shard_map/ppermute | solution.py:228
  82.0 2.0 %collective-permute-start.4 = (bf16[5120,256]{1,0:T(8,128)(2,1)}, bf16[5120,256]{1,0:T(8,128)(2,1)}, u32[]{:S(2)}, u32[]{:S(2)}) collective-permute-start(bf16[5120,256]{1,0:T(8,128)(2,1)} %wa_ref.1), channel_id=1, source_target_pairs={{0,1},{1,0},{2,3},{3,2},{4,5},{5,4},{6,7},{7,6},{8,9},{9,8},{10,11... | collective-permute-start | bytes 7864328 | tf_op jit(solution)/shard_map/ppermute | solution.py:228
  84.1 1.5 %shard_map.115 = (bf16[1,64,1280]{2,1,0:T(8,128)(2,1)}, bf16[8,64,1280]{2,1,0:T(8,128)(2,1)}) custom-call(f32[64,1280]{1,0:T(8,128)S(1)} %get-tuple-element.9.own_ref, f32[64,1280]{1,0:T(8,128)S(1)} %collective-permute-done.3.recv_ref, f32[1280]{0:T(1024)S(1)} %copy-done.3, f32[1280]{0:T(1024)S(1)} %copy-done.4), custom_call_target="tpu_custom_call" | custom-call | flops 4194304 | bytes 1048576 | tf_op jit(solution)/shard_map/pallas_call | solution.py:315
  85.6 3.6 %all-to-all-start.3 = ((bf16[8,64,1280]{2,1,0:T(8,128)(2,1)}), bf16[8,64,1280]{2,1,0:T(8,128)(2,1)S(1)}, u32[]{:S(2)}, u32[]{:S(2)}) async-start(bf16[8,64,1280]{2,1,0:T(8,128)(2,1)} %get-tuple-element.12), calls=%async_computation.3 | async-start | bytes 2621440 | tf_op jit(solution)/shard_map/all_to_all | solution.py:322
  89.1 34.7 %all-to-all-done.3.blocks_ref = bf16[8,64,1280]{2,1,0:T(8,128)(2,1)S(1)} async-done(((bf16[8,64,1280]{2,1,0:T(8,128)(2,1)}), bf16[8,64,1280]{2,1,0:T(8,128)(2,1)S(1)}, u32[]{:S(2)}, u32[]{:S(2)}) %all-to-all-start.3) | async-done | bytes 1310752 | tf_op jit(solution)/shard_map/all_to_all | solution.py:322
  123.9 1.7 %copy-done = bf16[5120,256]{1,0:T(8,128)(2,1)S(1)} copy-done((bf16[5120,256]{1,0:T(8,128)(2,1)S(1)}, bf16[5120,256]{1,0:T(8,128)(2,1)}, u32[]{:S(2)}) %copy-start) | copy-done | bytes 2621464
  125.6 2.8 %shard_map.116 = f32[16,128]{1,0:T(8,128)S(1)} custom-call(s32[1,4,2]{2,1,0:T(4,128)S(1)} %copy.17.grid_ref, s32[1,4]{1,0:T(1,128)S(1)} %copy-done.5, bf16[5120,256]{1,0:T(8,128)(2,1)S(1)} %copy-done, bf16[5120,256]{1,0:T(8,128)(2,1)} %collective-permute-done.4.wb_ref, bf16[8,64,1280]{2,1,0:T(8,128)(2,1)S(1)} %all-to-all-done.3.blocks_ref), custom_call_target="tpu_custom_call" | custom-call | flops 536870912 | bytes 7340032 | tf_op jit(solution)/shard_map/pallas_call | solution.py:330
  128.4 9.9 %all_to_all.31 = f32[16,1,128]{2,1,0:T(1,128)S(1)} all-to-all(f32[16,1,128]{2,1,0:T(1,128)S(1)} %bitcast.10), channel_id=1, replica_groups=mesh['rows'=32,'seq'=16] {'seq'}, dimensions={0} | all-to-all | bytes 16384 | tf_op jit(solution)/shard_map/all_to_all | solution.py:338
  138.3 1.2 shard_map.117
  (21 shorter events, 0.3 us)
Async XLA Ops:
  0.6 12.8 %copy-start.7 = (s32[1,4,2]{1,2,0:T(2,128)S(1)}, s32[1,4,2]{1,2,0:T(2,128)}, u32[]{:S(2)}) copy-start(s32[1,4,2]{1,2,0:T(2,128)} %param.13) | copy-start | bytes 100
  0.6 12.9 %copy-start.1 = (bf16[1,64,3840]{2,1,0:T(8,128)(2,1)S(1)}, bf16[1,64,3840]{2,1,0:T(8,128)(2,1)}, u32[]{:S(2)}) copy-start(bf16[1,64,3840]{2,1,0:T(8,128)(2,1)} %qkv_ref.1) | copy-start | bytes 1474564
  0.7 12.9 %copy-start.6 = (s32[1,64]{1,0:T(1,128)S(1)}, s32[1,64]{1,0:T(1,128)}, u32[]{:S(2)}) copy-start(s32[1,64]{1,0:T(1,128)} %keep_ref.1) | copy-start | bytes 772
  2.6 35.1 %all-to-all-start.2 = ((bf16[8,40,1280]{2,1,0:T(8,128)(2,1)}), bf16[8,40,1280]{2,1,0:T(8,128)(2,1)S(1)}, u32[]{:S(2)}, u32[]{:S(2)}) async-start(bf16[8,40,1280]{2,1,0:T(8,128)(2,1)} %broadcast_in_dim.2), calls=%async_computation.2 | async-start | bytes 1638400 | tf_op jit(solution)/shard_map/all_to_all | solution.py:233
  37.7 24.8 %all-to-all-start = ((bf16[16,64,256]{2,1,0:T(8,128)(2,1)}), bf16[16,64,256]{2,1,0:T(8,128)(2,1)S(1)}, u32[]{:S(2)}, u32[]{:S(2)}) async-start(bf16[16,64,256]{2,1,0:T(8,128)(2,1)} %shard_map.112), calls=%async_computation | async-start | bytes 1048576 | tf_op jit(solution)/shard_map/all_to_all | solution.py:288
  45.3 23.6 %collective-permute-start = (bf16[8,40,1280]{2,1,0:T(8,128)(2,1)S(1)}, bf16[8,40,1280]{2,1,0:T(8,128)(2,1)S(1)}, u32[]{:S(2)}, u32[]{:S(2)}) collective-permute-start(bf16[8,40,1280]{2,1,0:T(8,128)(2,1)S(1)} %all-to-all-done.2), channel_id=1, source_target_pairs={{0,16},{2,18},{4,20},{6,22},{8,24},{10,26},{12,28},{14,30},{16,32}... | collective-permute-start | bytes 2457608 | tf_op jit(solution)/shard_map/ppermute | solution.py:249
  46.6 22.9 %collective-permute-start.1 = (bf16[8,40,1280]{2,1,0:T(8,128)(2,1)S(1)}, bf16[8,40,1280]{2,1,0:T(8,128)(2,1)}, u32[]{:S(2)}, u32[]{:S(2)}) collective-permute-start(bf16[8,40,1280]{2,1,0:T(8,128)(2,1)S(1)} %all-to-all-done.2), channel_id=1, source_target_pairs={{0,32},{2,34},{4,36},{6,38},{8,40},{10,42},{12,44},{14,46},{16,48}... | collective-permute-start | bytes 2457608 | tf_op jit(solution)/shard_map/ppermute | solution.py:249
  47.9 21.6 %collective-permute-start.2 = (bf16[8,40,1280]{2,1,0:T(8,128)(2,1)S(1)}, bf16[8,40,1280]{2,1,0:T(8,128)(2,1)}, u32[]{:S(2)}, u32[]{:S(2)}) collective-permute-start(bf16[8,40,1280]{2,1,0:T(8,128)(2,1)S(1)} %all-to-all-done.2), channel_id=1, source_target_pairs={{0,48},{2,50},{4,52},{6,54},{8,56},{10,58},{12,60},{14,62},{16,0},... | collective-permute-start | bytes 2457608 | tf_op jit(solution)/shard_map/ppermute | solution.py:249
  65.5 13.6 %all-to-all-start.1 = ((bf16[8,80,128]{2,1,0:T(8,128)(2,1)}), bf16[8,80,128]{2,1,0:T(8,128)(2,1)S(1)}, u32[]{:S(2)}, u32[]{:S(2)}) async-start(bf16[8,80,128]{2,1,0:T(8,128)(2,1)} %shard_map.113), calls=%async_computation.1 | async-start | bytes 327680 | tf_op jit(solution)/shard_map/all_to_all | solution.py:298
  71.1 8.0 %copy-start.2 = (bf16[1,64,1280]{2,1,0:T(8,128)(2,1)S(1)}, bf16[1,64,1280]{2,1,0:T(8,128)(2,1)}, u32[]{:S(2)}) copy-start(bf16[1,64,1280]{2,1,0:T(8,128)(2,1)} %hidden_ref.1) | copy-start | bytes 491524
  71.2 12.8 %copy-start.3 = (f32[1280]{0:T(1024)S(1)}, f32[1280]{0:T(1024)}, u32[]{:S(2)}) copy-start(f32[1280]{0:T(1024)} %gain_ref.1) | copy-start | bytes 15364
  71.2 12.8 %copy-start.4 = (f32[1280]{0:T(1024)S(1)}, f32[1280]{0:T(1024)}, u32[]{:S(2)}) copy-start(f32[1280]{0:T(1024)} %bias_ref.1) | copy-start | bytes 15364
  79.7 4.3 %collective-permute-start.3 = (f32[64,1280]{1,0:T(8,128)S(1)}, f32[64,1280]{1,0:T(8,128)S(1)}, u32[]{:S(2)}, u32[]{:S(2)}) collective-permute-start(f32[64,1280]{1,0:T(8,128)S(1)} %get-tuple-element.10), channel_id=1, source_target_pairs={{0,1},{1,0},{2,3},{3,2},{4,5},{5,4},{6,7},{7,6},{8,9},{9,8},{10,11... | collective-permute-start | bytes 983048 | tf_op jit(solution)/shard_map/ppermute | solution.py:228
  82.0 7.2 %collective-permute-start.4 = (bf16[5120,256]{1,0:T(8,128)(2,1)}, bf16[5120,256]{1,0:T(8,128)(2,1)}, u32[]{:S(2)}, u32[]{:S(2)}) collective-permute-start(bf16[5120,256]{1,0:T(8,128)(2,1)} %wa_ref.1), channel_id=1, source_target_pairs={{0,1},{1,0},{2,3},{3,2},{4,5},{5,4},{6,7},{7,6},{8,9},{9,8},{10,11... | collective-permute-start | bytes 7864328 | tf_op jit(solution)/shard_map/ppermute | solution.py:228
  84.0 39.8 %copy-start.5 = (s32[1,4]{1,0:T(1,128)S(1)}, s32[1,4]{1,0:T(1,128)}, u32[]{:S(2)}) copy-start(s32[1,4]{1,0:T(1,128)} %owner_ref.3) | copy-start | bytes 52
  85.6 38.3 %all-to-all-start.3 = ((bf16[8,64,1280]{2,1,0:T(8,128)(2,1)}), bf16[8,64,1280]{2,1,0:T(8,128)(2,1)S(1)}, u32[]{:S(2)}, u32[]{:S(2)}) async-start(bf16[8,64,1280]{2,1,0:T(8,128)(2,1)} %get-tuple-element.12), calls=%async_computation.3 | async-start | bytes 2621440 | tf_op jit(solution)/shard_map/all_to_all | solution.py:322
  123.9 1.7 %copy-start = (bf16[5120,256]{1,0:T(8,128)(2,1)S(1)}, bf16[5120,256]{1,0:T(8,128)(2,1)}, u32[]{:S(2)}) copy-start(bf16[5120,256]{1,0:T(8,128)(2,1)} %wa_ref.1) | copy-start | bytes 7864324
where the time goes:
time: 140 us; the launch traced here: 139 us
  waiting for transfers between devices  77 us (55%)
  starting transfers between devices  33.9 us (24%)
  Pallas kernels  12.2 us (9%)
  blocking collectives  9.94 us (7%)
  local copies, waits for them, and re-layouts  3.77 us (3%)
  other arithmetic  1.75 us (1%)
    all_to_all x1, waiting for transfers between devices, body(): lax.all_to_all(blocks, 'seq', split_axis=0, concat_axis=0, axis_index_gro...  34.7 us
    all_to_all x1, waiting for transfers between devices, gather_weight(): lax.all_to_all(jnp.broadcast_to(weight[None], (8, 40, D)), 'rows', split_...  20.9 us
    all_to_all x1, waiting for transfers between devices, body(): lax.all_to_all(packed, 'seq', split_axis=0, concat_axis=0, tiled=True)  13 us
    all_to_all x1, starting transfers between devices, gather_weight(): lax.all_to_all(jnp.broadcast_to(weight[None], (8, 40, D)), 'rows', split_...  10.9 us
    all_to_all x1, blocking collectives, body(): lax.all_to_all(stats, 'seq', split_axis=0, concat_axis=0, tiled=True)  9.94 us
    all_to_all x1, waiting for transfers between devices, body(): lax.all_to_all(head_out, 'seq', split_axis=0, concat_axis=0, axis_index_g...  7.88 us
    all_to_all x1, starting transfers between devices, body(): lax.all_to_all(packed, 'seq', split_axis=0, concat_axis=0, tiled=True)  7.61 us
    ppermute x2, starting transfers between devices, chip_shift(): return lax.ppermute(x, 'seq', pairs)  4.33 us
  transfers between devices with their start and end apart: 9, of which 5 were waited for; matrix products, arithmetic and copies ran while one was open for 1% of the time, Pallas kernels for 6%

commit v1 on v0

--- a/solution.py
+++ b/solution.py
@@ -127,12 +127,16 @@
     emit(CHIPS - 1, x_ref[MAXIMG:SEQ, :].astype(F32))
 
 
-def mix_kernel(heads_ref, weight_ref, hidden_ref, own_ref, send_ref, part_ref):
+RING = (0, -1, 1, -2, 2, -3, 3, -4)
+
+
+def mix_kernel(heads_ref, hidden_ref, *refs):
+    own_ref, send_ref, part_ref = refs[CHIPS:]
+    z = lax.shift_right_logical(lax.axis_index("rows"), 2)
+    heads = jnp.concatenate([heads_ref[(z + step) & 7] for step in RING], axis=0)
+    weight = jnp.concatenate([ref[...] for ref in refs[:CHIPS]], axis=0)
     part_ref[...] = lax.dot_general(
-        heads_ref[...],
-        weight_ref[...],
-        (((0,), (0,)), ((), ())),
-        preferred_element_type=F32,
+        heads, weight, (((0,), (0,)), ((), ())), preferred_element_type=F32
     )
     core = lax.axis_index("seq") & 1
     mine = pl.multiple_of(core * TOK, TOK)
@@ -229,29 +233,21 @@
 
 
 def gather_weight(weight):
-    groups = [[z * 4 + x for z in range(8)] for x in range(4)]
-    column = lax.all_to_all(
-        jnp.broadcast_to(weight[None], (8, 40, D)),
-        "rows",
-        split_axis=0,
-        concat_axis=0,
-        axis_index_groups=groups,
-        tiled=True,
-    )
-
-    def shift_x(step, cores):
+    def shift_x(step):
         pairs = []
         for r in range(32):
             z, x = r // 4, r % 4
             for s in range(16):
-                if (x - 2 * (s % 2)) % 4 in cores:
+                if (x - 2 * (s % 2)) % 4 < 2:
                     pairs.append((r * 16 + s, (z * 4 + (x + step) % 4) * 16 + s))
-        return lax.ppermute(column, ("rows", "seq"), pairs)
-
-    two = shift_x(2, (0, 1))
-    plus = shift_x(1, (0, 1))
-    minus = shift_x(-1, (0, 1))
-    rel = (lax.axis_index("rows") - 2 * (lax.axis_index("seq") % 2)) % 4
+        return lax.ppermute(weight, ("rows", "seq"), pairs)
+
+    def shift_z(value, step):
+        pairs = [(r, (r + 4 * step) % 32) for r in range(32)]
+        return lax.ppermute(value, "rows", pairs)
+
+    two, plus, minus = shift_x(2), shift_x(1), shift_x(-1)
+    rel = (lax.axis_index("rows") - 2 * (lax.axis_index("seq") & 1)) & 3
 
     def pick(a, b, c, d):
         return jnp.where(
@@ -259,9 +255,16 @@
         )
 
     pair = jnp.concatenate(
-        [pick(column, plus, two, minus), pick(minus, column, plus, two)], axis=1
-    )
-    return pair.reshape(640, D)
+        [pick(weight, plus, two, minus), pick(minus, weight, plus, two)], axis=0
+    )
+    blocks = [pair]
+    up = down = pair
+    for _ in range(1, 4):
+        up = shift_z(up, 1)
+        down = shift_z(down, -1)
+        blocks += [up, down]
+    blocks.append(shift_z(up, 1))
+    return blocks
 
 
 def body(
@@ -302,15 +305,15 @@
         concat_axis=0,
         axis_index_groups=groups,
         tiled=True,
-    ).reshape(640, 128)
+    )
     own, send = call(
         mix_kernel,
         (shape((TOK, D), F32), shape((TOK, D), F32)),
-        [VM, VM, VM],
+        [VM] * (2 + CHIPS),
         scratch=[pltpu.VMEM((128, D), F32)],
         flops=1 << 28,
         bytes_accessed=3 << 20,
-    )(attended, weight, hidden)
+    )(attended, hidden, *weight)
     recv = chip_shift(send, 0, 1)
     normed, blocks = call(
         norm_kernel,
@@ -319,6 +322,7 @@
         flops=1 << 22,
         bytes_accessed=1 << 20,
     )(own, recv, norm_gain, norm_bias)
+    blocks, merge_other = lax.optimization_barrier((blocks, merge_other))
     blocks = lax.all_to_all(
         blocks,
         "seq",

time: 140 us -> 146 us (1.043)
  waiting for transfers between devices: 77 us -> 12.6 us
  blocking collectives: 9.94 us -> 51.6 us
  starting transfers between devices: 33.9 us -> 59.3 us
  local copies, waits for them, and re-layouts: 3.77 us -> 6.62 us
    all_to_all x2 -> x0, waiting for transfers between devices: 55.6 us -> none  [the longest x1 34.7 us: body(): lax.all_to_all(blocks, 'seq', split_axis=0, concat_axis=0, axis_index_gro...]
    all_to_all x0 -> x1, blocking collectives: none -> 40.4 us  [body(): lax.all_to_all(blocks, 'seq', split_axis=0, concat_axis=0, axis_index_gro...]
    ppermute x3 -> x10, starting transfers between devices: 4.19 us -> 30.9 us  [the longest x7 27.6 us: shift_z(): return lax.ppermute(value, 'rows', pairs)]
    all_to_all x2 -> x0, starting transfers between devices: 14.4 us -> none  [the longest x1 10.9 us: gather_weight(): lax.all_to_all(jnp.broadcast_to(weight[None], (8, 40, D)), 'rows', split_...]
    all_to_all x1, waiting for transfers between devices: 13 us -> 0.01 us  [body(): lax.all_to_all(packed, 'seq', split_axis=0, concat_axis=0, tiled=True)]
    ppermute x3 -> x10, waiting for transfers between devices: 0.54 us -> 11.3 us  [the longest x7 11.3 us: shift_z(): return lax.ppermute(value, 'rows', pairs)]
    ppermute x2, starting transfers between devices: 4.33 us -> 14.5 us  [chip_shift(): return lax.ppermute(x, 'seq', pairs)]
    all_to_all x1, waiting for transfers between devices: 7.88 us -> 0.01 us  [body(): lax.all_to_all(head_out, 'seq', split_axis=0, concat_axis=0, axis_index_g...]
  transfers between devices with their start and end apart: 9 -> 14, of which waited for: 5 -> 5; matrix products, arithmetic and copies ran while one was open for 1% -> 1% of each run, Pallas kernels for 6% -> 6%
where the time goes in v1:
time: 146 us; the launch traced here: 145 us
  starting transfers between devices  59.3 us (41%)
  blocking collectives  51.6 us (35%)
  Pallas kernels  12.8 us (9%)
  waiting for transfers between devices  12.6 us (9%)
  local copies, waits for them, and re-layouts  6.62 us (5%)
    all_to_all x1, blocking collectives, body(): lax.all_to_all(blocks, 'seq', split_axis=0, concat_axis=0, axis_index_gro...  40.4 us
    ppermute x7, starting transfers between devices, shift_z(): return lax.ppermute(value, 'rows', pairs)  27.6 us
    ppermute x2, starting transfers between devices, chip_shift(): return lax.ppermute(x, 'seq', pairs)  14.5 us
    ppermute x7, waiting for transfers between devices, shift_z(): return lax.ppermute(value, 'rows', pairs)  11.3 us
    all_to_all x1, blocking collectives, body(): lax.all_to_all(stats, 'seq', split_axis=0, concat_axis=0, tiled=True)  11.2 us
    all_to_all x1, starting transfers between devices, body(): lax.all_to_all(packed, 'seq', split_axis=0, concat_axis=0, tiled=True)  7.89 us
    unnamed x23, local copies, waits for them, and re-layouts  6.62 us
    all_to_all x1, starting transfers between devices, body(): lax.all_to_all(head_out, 'seq', split_axis=0, concat_axis=0, axis_index_g...  6.12 us
  transfers between devices with their start and end apart: 14, of which 5 were waited for; matrix products, arithmetic and copies ran while one was open for 1% of the time, Pallas kernels for 6%

profile of v1, /device:TPU:1, one launch (start us, length us, event | category | flops | bytes accessed | tf_op | source)
XLA Modules:
  0.0 144.8 jit_solution(16933865647778864572)
XLA Ops:
  0.6 8.8 %collective-permute-start.11 = (bf16[5120,256]{1,0:T(8,128)(2,1)}, bf16[5120,256]{1,0:T(8,128)(2,1)}, u32[]{:S(2)}, u32[]{:S(2)}) collective-permute-start(bf16[5120,256]{1,0:T(8,128)(2,1)} %wa_ref.1), channel_id=1, source_target_pairs={{0,1},{1,0},{2,3},{3,2},{4,5},{5,4},{6,7},{7,6},{8,9},{9,8},{10,11... | collective-permute-start | bytes 7864328 | tf_op jit(solution)/shard_map/ppermute | solution.py:232
  9.4 1.3 collective-permute-start.1
  10.7 1.3 collective-permute-start
  15.1 3.3 %shard_map.112 = bf16[16,64,256]{2,1,0:T(8,128)(2,1)} custom-call(s32[1,4,2]{2,1,0:T(4,128)S(1)} %copy.17.grid_ref, s32[1,64]{1,0:T(1,128)S(1)} %copy-done.10, bf16[1,64,3840]{2,1,0:T(8,128)(2,1)S(1)} %copy-done.1), custom_call_target="tpu_custom_call" | custom-call | flops 4194304 | bytes 1048576 | tf_op jit(solution)/shard_map/pallas_call | solution.py:284
  18.4 7.9 %all-to-all-start = ((bf16[16,64,256]{2,1,0:T(8,128)(2,1)}), bf16[16,64,256]{2,1,0:T(8,128)(2,1)S(1)}, u32[]{:S(2)}, u32[]{:S(2)}) async-start(bf16[16,64,256]{2,1,0:T(8,128)(2,1)} %shard_map.112), calls=%async_computation | async-start | bytes 1048576 | tf_op jit(solution)/shard_map/all_to_all | solution.py:291
  27.3 4.0 %collective-permute-start.3 = (bf16[80,1280]{1,0:T(8,128)(2,1)S(1)}, bf16[80,1280]{1,0:T(8,128)(2,1)S(1)}, u32[]{:S(2)}, u32[]{:S(2)}) collective-permute-start(bf16[80,1280]{1,0:T(8,128)(2,1)S(1)} %pad_maximum_fusion.refs_0_), channel_id=1, source_target_pairs={{0,64},{16,80},{32,96},{48,112},{64,128},{80,144},{96,160},{112,17... | collective-permute-start | bytes 614408 | tf_op jit(solution)/shard_map/ppermute | solution.py:247
  31.3 8.6 %collective-permute-start.4 = (bf16[80,1280]{1,0:T(8,128)(2,1)S(1)}, bf16[80,1280]{1,0:T(8,128)(2,1)S(1)}, u32[]{:S(2)}, u32[]{:S(2)}) collective-permute-start(bf16[80,1280]{1,0:T(8,128)(2,1)S(1)} %pad_maximum_fusion.refs_0_), channel_id=1, source_target_pairs={{0,448},{16,464},{32,480},{48,496},{64,0},{80,16},{96,32},{112,48}... | collective-permute-start | bytes 614408 | tf_op jit(solution)/shard_map/ppermute | solution.py:247
  39.9 3.4 %collective-permute-done.3.refs_1_ = bf16[80,1280]{1,0:T(8,128)(2,1)S(1)} collective-permute-done((bf16[80,1280]{1,0:T(8,128)(2,1)S(1)}, bf16[80,1280]{1,0:T(8,128)(2,1)S(1)}, u32[]{:S(2)}, u32[]{:S(2)}) %collective-permute-start.3) | collective-permute-done | bytes 204832 | tf_op jit(solution)/shard_map/ppermute | solution.py:247
  43.3 1.9 %collective-permute-start.5 = (bf16[80,1280]{1,0:T(8,128)(2,1)S(1)}, bf16[80,1280]{1,0:T(8,128)(2,1)}, u32[]{:S(2)}, u32[]{:S(2)}) collective-permute-start(bf16[80,1280]{1,0:T(8,128)(2,1)S(1)} %collective-permute-done.3.refs_1_), channel_id=1, source_target_pairs={{0,64},{16,80},{32,96},{48,112},{64,128},{80,144},{96,160},{112,17... | collective-permute-start | bytes 614408 | tf_op jit(solution)/shard_map/ppermute | solution.py:247
  45.2 4.6 %collective-permute-start.6 = (bf16[80,1280]{1,0:T(8,128)(2,1)S(1)}, bf16[80,1280]{1,0:T(8,128)(2,1)}, u32[]{:S(2)}, u32[]{:S(2)}) collective-permute-start(bf16[80,1280]{1,0:T(8,128)(2,1)S(1)} %collective-permute-done.4.refs_2_), channel_id=1, source_target_pairs={{0,448},{16,464},{32,480},{48,496},{64,0},{80,16},{96,32},{112,48}... | collective-permute-start | bytes 614408 | tf_op jit(solution)/shard_map/ppermute | solution.py:247
  49.8 2.6 %collective-permute-done.5.refs_3_ = bf16[80,1280]{1,0:T(8,128)(2,1)} collective-permute-done((bf16[80,1280]{1,0:T(8,128)(2,1)S(1)}, bf16[80,1280]{1,0:T(8,128)(2,1)}, u32[]{:S(2)}, u32[]{:S(2)}) %collective-permute-start.5) | collective-permute-done | bytes 204832 | tf_op jit(solution)/shard_map/ppermute | solution.py:247
  52.4 1.9 %collective-permute-start.7 = (bf16[80,1280]{1,0:T(8,128)(2,1)}, bf16[80,1280]{1,0:T(8,128)(2,1)}, u32[]{:S(2)}, u32[]{:S(2)}) collective-permute-start(bf16[80,1280]{1,0:T(8,128)(2,1)} %collective-permute-done.5.refs_3_), channel_id=1, source_target_pairs={{0,64},{16,80},{32,96},{48,112},{64,128},{80,144},{96,160},{112,17... | collective-permute-start | bytes 614408 | tf_op jit(solution)/shard_map/ppermute | solution.py:247
  54.4 3.0 %shard_map.113 = bf16[8,80,128]{2,1,0:T(8,128)(2,1)} custom-call(s32[1,4,2]{2,1,0:T(4,128)S(1)} %copy.17.grid_ref, bf16[1024,256]{1,0:T(8,128)(2,1)S(1)} %bitcast.5), custom_call_target="tpu_custom_call" | custom-call | flops 536870912 | bytes 1048576 | tf_op jit(solution)/shard_map/pallas_call | solution.py:293
  57.4 6.1 %all-to-all-start.1 = ((bf16[8,80,128]{2,1,0:T(8,128)(2,1)}), bf16[8,80,128]{2,1,0:T(8,128)(2,1)S(1)}, u32[]{:S(2)}, u32[]{:S(2)}) async-start(bf16[8,80,128]{2,1,0:T(8,128)(2,1)} %shard_map.113), calls=%async_computation.1 | async-start | bytes 327680 | tf_op jit(solution)/shard_map/all_to_all | solution.py:301
  63.5 4.7 %collective-permute-start.8 = (bf16[80,1280]{1,0:T(8,128)(2,1)}, bf16[80,1280]{1,0:T(8,128)(2,1)S(1)}, u32[]{:S(2)}, u32[]{:S(2)}) collective-permute-start(bf16[80,1280]{1,0:T(8,128)(2,1)} %collective-permute-done.6.refs_4_), channel_id=1, source_target_pairs={{0,448},{16,464},{32,480},{48,496},{64,0},{80,16},{96,32},{112,48}... | collective-permute-start | bytes 614408 | tf_op jit(solution)/shard_map/ppermute | solution.py:247
  68.2 1.9 %collective-permute-start.9 = (bf16[80,1280]{1,0:T(8,128)(2,1)}, bf16[80,1280]{1,0:T(8,128)(2,1)S(1)}, u32[]{:S(2)}, u32[]{:S(2)}) collective-permute-start(bf16[80,1280]{1,0:T(8,128)(2,1)} %collective-permute-done.7.refs_5_), channel_id=1, source_target_pairs={{0,64},{16,80},{32,96},{48,112},{64,128},{80,144},{96,160},{112,17... | collective-permute-start | bytes 614408 | tf_op jit(solution)/shard_map/ppermute | solution.py:247
  71.9 4.3 %collective-permute-done.9.refs_7_ = bf16[80,1280]{1,0:T(8,128)(2,1)S(1)} collective-permute-done((bf16[80,1280]{1,0:T(8,128)(2,1)}, bf16[80,1280]{1,0:T(8,128)(2,1)S(1)}, u32[]{:S(2)}, u32[]{:S(2)}) %collective-permute-start.9) | collective-permute-done | bytes 204832 | tf_op jit(solution)/shard_map/ppermute | solution.py:247
  79.6 1.7 %shard_map.114 = (f32[64,1280]{1,0:T(8,128)S(1)}, f32[64,1280]{1,0:T(8,128)S(1)}) custom-call(bf16[8,80,128]{2,1,0:T(8,128)(2,1)S(1)} %all-to-all-done.1.heads_ref, bf16[1,64,1280]{2,1,0:T(8,128)(2,1)S(1)} %copy-done.6, bf16[80,1280]{1,0:T(8,128)(2,1)S(1)} %pad_maximum_fusion.refs_0_, bf16[80,1280]{1,0:T(8,128)(2,1)S(1)} %collective-permute-done.3.refs_1_, ...), custom_call_target="tpu_custom_call" | custom-call | flops 268435456 | bytes 3145728 | tf_op jit(solution)/shard_map/pallas_call | solution.py:309
  81.3 5.7 %collective-permute-start.10 = (f32[64,1280]{1,0:T(8,128)S(1)}, f32[64,1280]{1,0:T(8,128)S(1)}, u32[]{:S(2)}, u32[]{:S(2)}) collective-permute-start(f32[64,1280]{1,0:T(8,128)S(1)} %get-tuple-element.12), channel_id=1, source_target_pairs={{0,1},{1,0},{2,3},{3,2},{4,5},{5,4},{6,7},{7,6},{8,9},{9,8},{10,11... | collective-permute-start | bytes 983048 | tf_op jit(solution)/shard_map/ppermute | solution.py:232
  87.0 1.2 collective-permute-done.10.recv_ref
  89.2 40.4 %all_to_all.26.blocks_ref = bf16[8,64,1280]{2,1,0:T(8,128)(2,1)S(1)} all-to-all(bf16[8,64,1280]{2,1,0:T(8,128)(2,1)S(1)} %get-tuple-element.16), channel_id=1, replica_groups={{0,2,4,6,8,10,12,14},{1,3,5,7,9,11,13,15},{16,18,20,22,24,26,28,30},{17..., dimensions={0} | all-to-all | bytes 2621440 | tf_op jit(solution)/shard_map/all_to_all | solution.py:326
  129.6 2.8 %shard_map.116 = f32[16,128]{1,0:T(8,128)S(1)} custom-call(s32[1,4,2]{2,1,0:T(4,128)S(1)} %copy.17.grid_ref, s32[1,4]{1,0:T(1,128)S(1)} %copy-done.9, bf16[5120,256]{1,0:T(8,128)(2,1)S(1)} %copy-done, bf16[5120,256]{1,0:T(8,128)(2,1)} %collective-permute-done.11.wb_ref, bf16[8,64,1280]{2,1,0:T(8,128)(2,1)S(1)} %all_to_all.26.blocks_ref), custom_call_target="tpu_custom_call" | custom-call | flops 536870912 | bytes 7340032 | tf_op jit(solution)/shard_map/pallas_call | solution.py:334
  132.4 11.2 %all_to_all.27 = f32[16,1,128]{2,1,0:T(1,128)S(1)} all-to-all(f32[16,1,128]{2,1,0:T(1,128)S(1)} %bitcast.6), channel_id=1, replica_groups=mesh['rows'=32,'seq'=16] {'seq'}, dimensions={0} | all-to-all | bytes 16384 | tf_op jit(solution)/shard_map/all_to_all | solution.py:342
  143.6 1.2 shard_map.117
  (37 shorter events, 10.2 us)
Async XLA Ops:
  0.6 88.6 %collective-permute-start.11 = (bf16[5120,256]{1,0:T(8,128)(2,1)}, bf16[5120,256]{1,0:T(8,128)(2,1)}, u32[]{:S(2)}, u32[]{:S(2)}) collective-permute-start(bf16[5120,256]{1,0:T(8,128)(2,1)} %wa_ref.1), channel_id=1, source_target_pairs={{0,1},{1,0},{2,3},{3,2},{4,5},{5,4},{6,7},{7,6},{8,9},{9,8},{10,11... | collective-permute-start | bytes 7864328 | tf_op jit(solution)/shard_map/ppermute | solution.py:232
  9.4 16.9 %collective-permute-start.1 = (bf16[40,1280]{1,0:T(8,128)(2,1)}, bf16[40,1280]{1,0:T(8,128)(2,1)S(1)}, u32[]{:S(2)}, u32[]{:S(2)}) collective-permute-start(bf16[40,1280]{1,0:T(8,128)(2,1)} %param.15), channel_id=1, source_target_pairs={{0,32},{2,34},{4,36},{6,38},{8,40},{10,42},{12,44},{14,46},{16,48}... | collective-permute-start | bytes 307208 | tf_op jit(solution)/shard_map/ppermute | solution.py:243
  10.7 15.6 %collective-permute-start = (bf16[40,1280]{1,0:T(8,128)(2,1)}, bf16[40,1280]{1,0:T(8,128)(2,1)S(1)}, u32[]{:S(2)}, u32[]{:S(2)}) collective-permute-start(bf16[40,1280]{1,0:T(8,128)(2,1)} %param.15), channel_id=1, source_target_pairs={{0,16},{2,18},{4,20},{6,22},{8,24},{10,26},{12,28},{14,30},{16,32}... | collective-permute-start | bytes 307208 | tf_op jit(solution)/shard_map/ppermute | solution.py:243
  12.0 14.4 %collective-permute-start.2 = (bf16[40,1280]{1,0:T(8,128)(2,1)}, bf16[40,1280]{1,0:T(8,128)(2,1)S(1)}, u32[]{:S(2)}, u32[]{:S(2)}) collective-permute-start(bf16[40,1280]{1,0:T(8,128)(2,1)} %param.15), channel_id=1, source_target_pairs={{0,48},{2,50},{4,52},{6,54},{8,56},{10,58},{12,60},{14,62},{16,0},... | collective-permute-start | bytes 307208 | tf_op jit(solution)/shard_map/ppermute | solution.py:243
  13.4 1.0 copy-start.1
  18.4 36.0 %all-to-all-start = ((bf16[16,64,256]{2,1,0:T(8,128)(2,1)}), bf16[16,64,256]{2,1,0:T(8,128)(2,1)S(1)}, u32[]{:S(2)}, u32[]{:S(2)}) async-start(bf16[16,64,256]{2,1,0:T(8,128)(2,1)} %shard_map.112), calls=%async_computation | async-start | bytes 1048576 | tf_op jit(solution)/shard_map/all_to_all | solution.py:291
  26.3 62.0 %copy-start.7 = (f32[1280]{0:T(1024)S(1)}, f32[1280]{0:T(1024)}, u32[]{:S(2)}) copy-start(f32[1280]{0:T(1024)} %gain_ref.1) | copy-start | bytes 15364
  26.3 62.0 %copy-start.8 = (f32[1280]{0:T(1024)S(1)}, f32[1280]{0:T(1024)}, u32[]{:S(2)}) copy-start(f32[1280]{0:T(1024)} %bias_ref.1) | copy-start | bytes 15364
  27.3 16.0 %collective-permute-start.3 = (bf16[80,1280]{1,0:T(8,128)(2,1)S(1)}, bf16[80,1280]{1,0:T(8,128)(2,1)S(1)}, u32[]{:S(2)}, u32[]{:S(2)}) collective-permute-start(bf16[80,1280]{1,0:T(8,128)(2,1)S(1)} %pad_maximum_fusion.refs_0_), channel_id=1, source_target_pairs={{0,64},{16,80},{32,96},{48,112},{64,128},{80,144},{96,160},{112,17... | collective-permute-start | bytes 614408 | tf_op jit(solution)/shard_map/ppermute | solution.py:247
  31.3 13.9 %collective-permute-start.4 = (bf16[80,1280]{1,0:T(8,128)(2,1)S(1)}, bf16[80,1280]{1,0:T(8,128)(2,1)S(1)}, u32[]{:S(2)}, u32[]{:S(2)}) collective-permute-start(bf16[80,1280]{1,0:T(8,128)(2,1)S(1)} %pad_maximum_fusion.refs_0_), channel_id=1, source_target_pairs={{0,448},{16,464},{32,480},{48,496},{64,0},{80,16},{96,32},{112,48}... | collective-permute-start | bytes 614408 | tf_op jit(solution)/shard_map/ppermute | solution.py:247
  43.3 9.1 %collective-permute-start.5 = (bf16[80,1280]{1,0:T(8,128)(2,1)S(1)}, bf16[80,1280]{1,0:T(8,128)(2,1)}, u32[]{:S(2)}, u32[]{:S(2)}) collective-permute-start(bf16[80,1280]{1,0:T(8,128)(2,1)S(1)} %collective-permute-done.3.refs_1_), channel_id=1, source_target_pairs={{0,64},{16,80},{32,96},{48,112},{64,128},{80,144},{96,160},{112,17... | collective-permute-start | bytes 614408 | tf_op jit(solution)/shard_map/ppermute | solution.py:247
  45.2 18.3 %collective-permute-start.6 = (bf16[80,1280]{1,0:T(8,128)(2,1)S(1)}, bf16[80,1280]{1,0:T(8,128)(2,1)}, u32[]{:S(2)}, u32[]{:S(2)}) collective-permute-start(bf16[80,1280]{1,0:T(8,128)(2,1)S(1)} %collective-permute-done.4.refs_2_), channel_id=1, source_target_pairs={{0,448},{16,464},{32,480},{48,496},{64,0},{80,16},{96,32},{112,48}... | collective-permute-start | bytes 614408 | tf_op jit(solution)/shard_map/ppermute | solution.py:247
  52.4 15.8 %collective-permute-start.7 = (bf16[80,1280]{1,0:T(8,128)(2,1)}, bf16[80,1280]{1,0:T(8,128)(2,1)}, u32[]{:S(2)}, u32[]{:S(2)}) collective-permute-start(bf16[80,1280]{1,0:T(8,128)(2,1)} %collective-permute-done.5.refs_3_), channel_id=1, source_target_pairs={{0,64},{16,80},{32,96},{48,112},{64,128},{80,144},{96,160},{112,17... | collective-permute-start | bytes 614408 | tf_op jit(solution)/shard_map/ppermute | solution.py:247
  57.4 72.2 %copy-start.9 = (s32[1,4]{1,0:T(1,128)S(1)}, s32[1,4]{1,0:T(1,128)}, u32[]{:S(2)}) copy-start(s32[1,4]{1,0:T(1,128)} %owner_ref.3) | copy-start | bytes 52
  57.4 19.5 %all-to-all-start.1 = ((bf16[8,80,128]{2,1,0:T(8,128)(2,1)}), bf16[8,80,128]{2,1,0:T(8,128)(2,1)S(1)}, u32[]{:S(2)}, u32[]{:S(2)}) async-start(bf16[8,80,128]{2,1,0:T(8,128)(2,1)} %shard_map.113), calls=%async_computation.1 | async-start | bytes 327680 | tf_op jit(solution)/shard_map/all_to_all | solution.py:301
  63.5 66.1 %copy-start = (bf16[5120,256]{1,0:T(8,128)(2,1)S(1)}, bf16[5120,256]{1,0:T(8,128)(2,1)}, u32[]{:S(2)}) copy-start(bf16[5120,256]{1,0:T(8,128)(2,1)} %wa_ref.1) | copy-start | bytes 7864324
  63.5 7.7 %collective-permute-start.8 = (bf16[80,1280]{1,0:T(8,128)(2,1)}, bf16[80,1280]{1,0:T(8,128)(2,1)S(1)}, u32[]{:S(2)}, u32[]{:S(2)}) collective-permute-start(bf16[80,1280]{1,0:T(8,128)(2,1)} %collective-permute-done.6.refs_4_), channel_id=1, source_target_pairs={{0,448},{16,464},{32,480},{48,496},{64,0},{80,16},{96,32},{112,48}... | collective-permute-start | bytes 614408 | tf_op jit(solution)/shard_map/ppermute | solution.py:247
  68.2 7.9 %collective-permute-start.9 = (bf16[80,1280]{1,0:T(8,128)(2,1)}, bf16[80,1280]{1,0:T(8,128)(2,1)S(1)}, u32[]{:S(2)}, u32[]{:S(2)}) collective-permute-start(bf16[80,1280]{1,0:T(8,128)(2,1)} %collective-permute-done.7.refs_5_), channel_id=1, source_target_pairs={{0,64},{16,80},{32,96},{48,112},{64,128},{80,144},{96,160},{112,17... | collective-permute-start | bytes 614408 | tf_op jit(solution)/shard_map/ppermute | solution.py:247
  71.2 0.7 copy-start.2
  76.2 0.7 copy-start.4
  76.9 0.9 copy-start.3
  77.8 0.9 copy-start.5
  78.7 0.9 copy-start.6
  81.3 7.0 %collective-permute-start.10 = (f32[64,1280]{1,0:T(8,128)S(1)}, f32[64,1280]{1,0:T(8,128)S(1)}, u32[]{:S(2)}, u32[]{:S(2)}) collective-permute-start(f32[64,1280]{1,0:T(8,128)S(1)} %get-tuple-element.12), channel_id=1, source_target_pairs={{0,1},{1,0},{2,3},{3,2},{4,5},{5,4},{6,7},{7,6},{8,9},{9,8},{10,11... | collective-permute-start | bytes 983048 | tf_op jit(solution)/shard_map/ppermute | solution.py:232
  (1 other events, 0.7 us)

commit v2 on v1

--- a/solution.py
+++ b/solution.py
@@ -33,7 +33,7 @@
     starts, ends, total = [], [], 0
     for j in range(IMGS):
         starts.append(total)
-        total = total + grid_ref[0, j, 0] * grid_ref[0, j, 1]
+        total = total + grid_ref[0, 0, j] * grid_ref[0, 1, j]
         ends.append(total)
     return starts, ends
 
@@ -46,7 +46,7 @@
     for j in range(IMGS):
         inside = (place >= starts[j]) & (place < ends[j])
         begin = jnp.where(inside, starts[j], begin)
-        width = jnp.where(inside, grid_ref[0, j, 1], width)
+        width = jnp.where(inside, grid_ref[0, 1, j], width)
     valid = place < ends[IMGS - 1]
     offset = place - begin
     square = lax.shift_right_logical(offset, 2)
@@ -71,10 +71,16 @@
     diagonal = iota((TOK, TOK), 0) == iota((TOK, TOK), 1)
     flags = jnp.where(diagonal, keep_ref[...].astype(F32), 0.0)
     tail = jnp.broadcast_to(jnp.sum(flags, axis=1, keepdims=True), (TOK, 16))
-    for dest in range(HEADS):
-        q = qkv_ref[0, :, dest * HD : dest * HD + HD].astype(F32)
-        k = qkv_ref[0, :, D + dest * HD : D + dest * HD + HD].astype(F32)
-        v = qkv_ref[0, :, 2 * D + dest * HD : 2 * D + dest * HD + HD].astype(F32)
+    z = lax.shift_right_logical(lax.axis_index("rows"), 2)
+    for head in range(HEADS):
+        behind = (z - head // 2) & 7
+        ahead = (head // 2 - z) & 7
+        low_core = (behind >= 1) & (behind <= 4)
+        place = jnp.where(low_core, behind - 1, (ahead + 3) & 3) + 4 * (head % 2)
+        dest = 2 * place + jnp.where(low_core, 0, 1)
+        q = qkv_ref[0, :, head * HD : head * HD + HD].astype(F32)
+        k = qkv_ref[0, :, D + head * HD : D + head * HD + HD].astype(F32)
+        v = qkv_ref[0, :, 2 * D + head * HD : 2 * D + head * HD + HD].astype(F32)
         full = jnp.concatenate([q, v[:, :48], k, v[:, 48:], tail], axis=1)
         swapped = jnp.where(low, pltpu.roll(full, 256 - 20, 1), pltpu.roll(full, 20, 1))
         out_ref[dest] = (full * cosine + swapped * sine).astype(BF16)
@@ -127,47 +133,51 @@
     emit(CHIPS - 1, x_ref[MAXIMG:SEQ, :].astype(F32))
 
 
-RING = (0, -1, 1, -2, 2, -3, 3, -4)
+def take_four(refs):
+    core = lax.axis_index("seq") & 1
+    own_ref, one, two, three, four_ref = refs
+    fourth = jnp.where(core == 0, four_ref[...], own_ref[...])
+    return [one[...], two[...], three[...], fourth]
 
 
 def mix_kernel(heads_ref, hidden_ref, *refs):
-    own_ref, send_ref, part_ref = refs[CHIPS:]
-    z = lax.shift_right_logical(lax.axis_index("rows"), 2)
-    heads = jnp.concatenate([heads_ref[(z + step) & 7] for step in RING], axis=0)
-    weight = jnp.concatenate([ref[...] for ref in refs[:CHIPS]], axis=0)
-    part_ref[...] = lax.dot_general(
+    out_ref = refs[5]
+    core = lax.axis_index("seq") & 1
+    heads = jnp.concatenate(
+        [heads_ref[i + 4 * half] for i in range(4) for half in range(2)], axis=0
+    )
+    weight = jnp.concatenate(take_four(refs[:5]), axis=0)
+    out_ref[...] = lax.dot_general(
         heads, weight, (((0,), (0,)), ((), ())), preferred_element_type=F32
     )
-    core = lax.axis_index("seq") & 1
-    mine = pl.multiple_of(core * TOK, TOK)
-    other = pl.multiple_of((1 - core) * TOK, TOK)
-    own_ref[...] = part_ref[pl.ds(mine, TOK), :] + hidden_ref[0].astype(F32)
-    send_ref[...] = part_ref[pl.ds(other, TOK), :]
-
-
-def norm_kernel(own_ref, recv_ref, gain_ref, bias_ref, normed_ref, block_ref):
+    mine = pl.ds(pl.multiple_of(core * TOK, TOK), TOK)
+    out_ref[mine, :] = out_ref[mine, :] + hidden_ref[0].astype(F32)
+
+
+def norm_kernel(own_ref, recv_ref, gain_ref, bias_ref, normed_ref, block_ref, keep_ref):
     mixed = own_ref[...] + recv_ref[...]
     centred = mixed - jnp.mean(mixed, axis=1, keepdims=True)
     spread = jnp.mean(centred * centred, axis=1, keepdims=True)
-    normed = centred * lax.rsqrt(spread + 1e-05) * gain_ref[...].reshape(1, D) + bias_ref[...].reshape(1, D)
-    normed = normed.astype(BF16)
-    normed_ref[0] = normed
-    line = iota((TOK, TOK), 0)
-    source = 4 * (line & 15) + lax.shift_right_logical(line, 4)
-    order = jnp.where(iota((TOK, TOK), 1) == source, 1.0, 0.0).astype(BF16)
-    block = jnp.dot(order, normed, preferred_element_type=F32).astype(BF16)
-    for chip in range(CHIPS):
-        block_ref[chip] = block
-
-
-def project_kernel(grid_ref, owner_ref, wa_ref, wb_ref, blocks_ref, out_ref):
+    normed = centred * lax.rsqrt(spread + 1e-05) * gain_ref[...].reshape(1, D)
+    normed = (normed + bias_ref[...].reshape(1, D)).astype(BF16)
+    keep_ref[...] = normed
+    core = lax.axis_index("seq") & 1
+    normed_ref[0] = keep_ref[pl.ds(pl.multiple_of(core * TOK, TOK), TOK), :]
+    line = iota((128, 128), 0)
+    source = 4 * (line & 31) + lax.shift_right_logical(line, 5)
+    order = jnp.where(iota((128, 128), 1) == source, 1.0, 0.0).astype(BF16)
+    block_ref[...] = jnp.dot(order, normed, preferred_element_type=F32).astype(BF16)
+
+
+def project_kernel(grid_ref, owner_ref, wa_ref, wb_ref, *refs):
+    out_ref = refs[5]
+    bundles = take_four(refs[:5])
     halves = []
     for w_ref in (wa_ref, wb_ref):
         part = 0.0
         for corner in range(4):
             rows = jnp.concatenate(
-                [blocks_ref[c, 16 * corner : 16 * corner + 16, :] for c in range(CHIPS)],
-                axis=0,
+                [b[32 * corner : 32 * corner + 32, :] for b in bundles], axis=0
             )
             part = part + jnp.dot(
                 rows, w_ref[D * corner : D * corner + D, :], preferred_element_type=F32
@@ -178,8 +188,11 @@
     peaks = jnp.max(done, axis=1, keepdims=True)
     _, ends = image_bounds(grid_ref)
     line = iota((128, 128), 0)
-    source = 2 * lax.shift_right_logical(line, 4) + (lax.axis_index("seq") & 1)
-    token = source * TOK + 4 * (line & 15)
+    index = lax.axis_index("seq")
+    step = lax.shift_right_logical(line, 5) + 1
+    step = jnp.where((index & 1) == 0, -step, step & 3)
+    source = (lax.shift_right_logical(index, 1) + step) & 7
+    token = source * 128 + 4 * (line & 31)
     slot = jnp.full((128, 128), -1, jnp.int32)
     for j in reversed(range(IMGS)):
         slot = jnp.where(token < ends[j], owner_ref[0, j], slot)
@@ -197,7 +210,7 @@
     me = lax.axis_index("seq")
     count = 0
     for j in range(IMGS):
-        size = lax.shift_right_logical(grid_ref[0, j, 0] * grid_ref[0, j, 1], 2)
+        size = lax.shift_right_logical(grid_ref[0, 0, j] * grid_ref[0, 1, j], 2)
         count = count + jnp.where(owner_ref[0, j] == me, size, 0)
     counts = jnp.full((1, 1), count, jnp.int32)
     divisor = (jnp.maximum(counts, 1) * OUT).astype(F32)
@@ -232,39 +245,43 @@
     return lax.ppermute(x, "seq", pairs)
 
 
+def two_way(axes, value, move, count):
+    bundles = [value]
+    for k in range(1, 5):
+        pairs = []
+        for index in range(count):
+            core = index & 1
+            if k < 4 or core == 0:
+                pairs.append((index, move(index, 1 - 2 * core)))
+        value = lax.ppermute(value, axes, pairs)
+        bundles.append(value)
+    return bundles
+
+
 def gather_weight(weight):
     def shift_x(step):
-        pairs = []
-        for r in range(32):
-            z, x = r // 4, r % 4
-            for s in range(16):
-                if (x - 2 * (s % 2)) % 4 < 2:
-                    pairs.append((r * 16 + s, (z * 4 + (x + step) % 4) * 16 + s))
-        return lax.ppermute(weight, ("rows", "seq"), pairs)
-
-    def shift_z(value, step):
-        pairs = [(r, (r + 4 * step) % 32) for r in range(32)]
-        return lax.ppermute(value, "rows", pairs)
+        pairs = [(r, (r & ~3) + ((r + step) & 3)) for r in range(32)]
+        return lax.ppermute(weight, "rows", pairs)
 
     two, plus, minus = shift_x(2), shift_x(1), shift_x(-1)
-    rel = (lax.axis_index("rows") - 2 * (lax.axis_index("seq") & 1)) & 3
-
-    def pick(a, b, c, d):
-        return jnp.where(
-            rel == 0, a, jnp.where(rel == 1, b, jnp.where(rel == 2, c, d))
+    here = lax.axis_index("rows") & 3
+    parts = []
+    for x in range(4):
+        rel = (x - here) & 3
+        parts.append(
+            jnp.where(
+                rel == 0,
+                weight,
+                jnp.where(rel == 1, minus, jnp.where(rel == 2, two, plus)),
+            )
         )
-
-    pair = jnp.concatenate(
-        [pick(weight, plus, two, minus), pick(minus, weight, plus, two)], axis=0
-    )
-    blocks = [pair]
-    up = down = pair
-    for _ in range(1, 4):
-        up = shift_z(up, 1)
-        down = shift_z(down, -1)
-        blocks += [up, down]
-    blocks.append(shift_z(up, 1))
-    return blocks
+    bundle = jnp.concatenate(parts, axis=0)
+
+    def move(index, step):
+        row, place = index // 16, index % 16
+        return (row + 4 * step) % 32 * 16 + place
+
+    return two_way(("rows", "seq"), bundle, move, 512)
 
 
 def body(
@@ -280,6 +297,7 @@
     merge_weight,
 ):
     del segment_ids
+    grid_sizes = jnp.transpose(grid_sizes, (0, 2, 1))
     weight = gather_weight(out_weight)
     packed = call(
         rotary_kernel,
@@ -287,6 +305,7 @@
         [SM, VM, VM],
         flops=1 << 22,
         bytes_accessed=1 << 20,
+        mib=56,
     )(grid_sizes, key_keep, qkv)
     heads_all = lax.all_to_all(packed, "seq", split_axis=0, concat_axis=0, tiled=True)
     merge_other = chip_shift(merge_weight, 0, 1)
@@ -306,39 +325,35 @@
         axis_index_groups=groups,
         tiled=True,
     )
-    own, send = call(
+    mixed = call(
         mix_kernel,
-        (shape((TOK, D), F32), shape((TOK, D), F32)),
-        [VM] * (2 + CHIPS),
-        scratch=[pltpu.VMEM((128, D), F32)],
+        shape((128, D), F32),
+        [VM] * 7,
         flops=1 << 28,
         bytes_accessed=3 << 20,
     )(attended, hidden, *weight)
-    recv = chip_shift(send, 0, 1)
-    normed, blocks = call(
+    recv = chip_shift(mixed, 0, 1)
+    normed, block = call(
         norm_kernel,
-        (shape((1, TOK, D), BF16), shape((CHIPS, TOK, D), BF16)),
+        (shape((1, TOK, D), BF16), shape((128, D), BF16)),
         [VM] * 4,
+        scratch=[pltpu.VMEM((128, D), BF16)],
         flops=1 << 22,
         bytes_accessed=1 << 20,
-    )(own, recv, norm_gain, norm_bias)
-    blocks, merge_other = lax.optimization_barrier((blocks, merge_other))
-    blocks = lax.all_to_all(
-        blocks,
-        "seq",
-        split_axis=0,
-        concat_axis=0,
-        axis_index_groups=groups,
-        tiled=True,
-    )
+    )(mixed, recv, norm_gain, norm_bias)
+
+    def move(index, step):
+        return (index + 2 * step) % 16
+
+    bundles = two_way("seq", block, move, 16)
     stats = call(
         project_kernel,
         shape((16, 128), F32),
-        [SM, SM, VM, VM, VM],
+        [SM, SM] + [VM] * 7,
         flops=1 << 29,
         bytes_accessed=7 << 20,
         mib=16,
-    )(grid_sizes, owner_slots, merge_weight, merge_other, blocks)
+    )(grid_sizes, owner_slots, merge_weight, merge_other, *bundles)
     stats = lax.all_to_all(stats, "seq", split_axis=0, concat_axis=0, tiled=True)
     norm, peak = call(
         final_kernel, (shape((1, 1), F32), shape((1, 1), F32)), [SM, SM, VM]

time: 146 us -> 146 us (level)
  waiting for transfers between devices: 12.6 us -> 29.3 us
  blocking collectives: 51.6 us -> 40.5 us
  local copies, waits for them, and re-layouts: 6.62 us -> 3.4 us
  starting transfers between devices: 59.3 us -> 57.5 us
    all_to_all x1, blocking collectives: 40.4 us -> 14.6 us  [body(): lax.all_to_all(head_out, 'seq', split_axis=0, concat_axis=0, axis_index_g...]
    ppermute x10 -> x11, waiting for transfers between devices: 11.3 us -> 27.6 us  [the longest x8 22.5 us: two_way(): value = lax.ppermute(value, axes, pairs)]
    all_to_all x1, blocking collectives: 11.2 us -> 25.8 us  [body(): lax.all_to_all(stats, 'seq', split_axis=0, concat_axis=0, tiled=True)]
    ppermute x10 -> x11, starting transfers between devices: 30.9 us -> 41.2 us  [the longest x8 30.2 us: two_way(): value = lax.ppermute(value, axes, pairs)]
    all_to_all x1 -> x0, starting transfers between devices: 6.12 us -> none  [body(): lax.all_to_all(head_out, 'seq', split_axis=0, concat_axis=0, axis_index_g...]
    ppermute x2, starting transfers between devices: 14.5 us -> 9.08 us  [chip_shift(): return lax.ppermute(x, 'seq', pairs)]
    unnamed x23 -> x18, local copies, waits for them, and re-layouts: 6.62 us -> 3.4 us
  transfers between devices with their start and end apart: 14 -> 14, of which waited for: 5 -> 8; matrix products, arithmetic and copies ran while one was open for 1% -> 0% of each run, Pallas kernels for 6% -> 6%
where the time goes in v2:
time: 146 us; the launch traced here: 145 us
  starting transfers between devices  57.5 us (39%)
  blocking collectives  40.5 us (28%)
  waiting for transfers between devices  29.3 us (20%)
  Pallas kernels  12.8 us (9%)
  local copies, waits for them, and re-layouts  3.4 us (2%)
    ppermute x8, starting transfers between devices, two_way(): value = lax.ppermute(value, axes, pairs)  30.2 us
    all_to_all x1, blocking collectives, body(): lax.all_to_all(stats, 'seq', split_axis=0, concat_axis=0, tiled=True)  25.8 us
    ppermute x8, waiting for transfers between devices, two_way(): value = lax.ppermute(value, axes, pairs)  22.5 us
    all_to_all x1, blocking collectives, body(): lax.all_to_all(head_out, 'seq', split_axis=0, concat_axis=0, axis_index_g...  14.6 us
    ppermute x3, starting transfers between devices, shift_x(): return lax.ppermute(weight, 'rows', pairs)  11 us
    ppermute x2, starting transfers between devices, chip_shift(): return lax.ppermute(x, 'seq', pairs)  9.08 us
    all_to_all x1, starting transfers between devices, body(): lax.all_to_all(packed, 'seq', split_axis=0, concat_axis=0, tiled=True)  7.23 us
    ppermute x3, waiting for transfers between devices, shift_x(): return lax.ppermute(weight, 'rows', pairs)  5.04 us
  transfers between devices with their start and end apart: 14, of which 8 were waited for; matrix products, arithmetic and copies ran while one was open for 0% of the time, Pallas kernels for 6%

profile of v2, /device:TPU:1, one launch (start us, length us, event | category | flops | bytes accessed | tf_op | source)
XLA Modules:
  0.0 145.3 jit_solution(16584084815459953302)
XLA Ops:
  0.6 5.7 %collective-permute-start.1 = (bf16[40,1280]{1,0:T(8,128)(2,1)}, bf16[40,1280]{1,0:T(8,128)(2,1)S(1)}, u32[]{:S(2)}, u32[]{:S(2)}) collective-permute-start(bf16[40,1280]{1,0:T(8,128)(2,1)} %param.15), channel_id=1, source_target_pairs={{0,32},{16,48},{32,0},{48,16},{64,96},{80,112},{96,64},{112,80},{1... | collective-permute-start | bytes 307208 | tf_op jit(solution)/shard_map/ppermute | solution.py:264
  6.4 2.8 %collective-permute-start = (bf16[40,1280]{1,0:T(8,128)(2,1)}, bf16[40,1280]{1,0:T(8,128)(2,1)S(1)}, u32[]{:S(2)}, u32[]{:S(2)}) collective-permute-start(bf16[40,1280]{1,0:T(8,128)(2,1)} %param.15), channel_id=1, source_target_pairs={{0,48},{16,0},{32,16},{48,32},{64,112},{80,64},{96,80},{112,96},{1... | collective-permute-start | bytes 307208 | tf_op jit(solution)/shard_map/ppermute | solution.py:264
  9.2 2.5 %collective-permute-start.2 = (bf16[40,1280]{1,0:T(8,128)(2,1)}, bf16[40,1280]{1,0:T(8,128)(2,1)S(1)}, u32[]{:S(2)}, u32[]{:S(2)}) collective-permute-start(bf16[40,1280]{1,0:T(8,128)(2,1)} %param.15), channel_id=1, source_target_pairs={{0,16},{16,32},{32,48},{48,0},{64,80},{80,96},{96,112},{112,64},{1... | collective-permute-start | bytes 307208 | tf_op jit(solution)/shard_map/ppermute | solution.py:264
  12.0 4.8 %collective-permute-done.2 = bf16[40,1280]{1,0:T(8,128)(2,1)S(1)} collective-permute-done((bf16[40,1280]{1,0:T(8,128)(2,1)}, bf16[40,1280]{1,0:T(8,128)(2,1)S(1)}, u32[]{:S(2)}, u32[]{:S(2)}) %collective-permute-start.2) | collective-permute-done | bytes 102432 | tf_op jit(solution)/shard_map/ppermute | solution.py:264
  17.7 9.9 %collective-permute-start.3 = (bf16[160,1280]{1,0:T(8,128)(2,1)S(1)}, bf16[160,1280]{1,0:T(8,128)(2,1)}, u32[]{:S(2)}, u32[]{:S(2)}) collective-permute-start(bf16[160,1280]{1,0:T(8,128)(2,1)S(1)} %pad_maximum_fusion.refs_0_), channel_id=1, source_target_pairs={{0,64},{1,449},{2,66},{3,451},{4,68},{5,453},{6,70},{7,455},{8,72}... | collective-permute-start | bytes 1228808 | tf_op jit(solution)/shard_map/ppermute | solution.py:256
  27.6 3.8 %shard_map.112 = bf16[16,64,256]{2,1,0:T(8,128)(2,1)} custom-call(s32[1,2,4]{2,1,0:T(2,128)} %bitcast.9, s32[1,64]{1,0:T(1,128)} %keep_ref.1, bf16[1,64,3840]{2,1,0:T(8,128)(2,1)} %qkv_ref.1), custom_call_target="tpu_custom_call" | custom-call | flops 4194304 | bytes 1048576 | tf_op jit(solution)/shard_map/pallas_call | solution.py:302
  31.4 7.2 %all-to-all-start = ((bf16[16,64,256]{2,1,0:T(8,128)(2,1)}), bf16[16,64,256]{2,1,0:T(8,128)(2,1)S(1)}, u32[]{:S(2)}, u32[]{:S(2)}) async-start(bf16[16,64,256]{2,1,0:T(8,128)(2,1)} %shard_map.112), calls=%async_computation | async-start | bytes 1048576 | tf_op jit(solution)/shard_map/all_to_all | solution.py:310
  38.7 4.2 %collective-permute-start.4 = (bf16[160,1280]{1,0:T(8,128)(2,1)}, bf16[160,1280]{1,0:T(8,128)(2,1)S(1)}, u32[]{:S(2)}, u32[]{:S(2)}) collective-permute-start(bf16[160,1280]{1,0:T(8,128)(2,1)} %collective-permute-done.3.refs_1_), channel_id=1, source_target_pairs={{0,64},{1,449},{2,66},{3,451},{4,68},{5,453},{6,70},{7,455},{8,72}... | collective-permute-start | bytes 1228808 | tf_op jit(solution)/shard_map/ppermute | solution.py:256
  42.9 5.2 %collective-permute-done.4.refs_2_ = bf16[160,1280]{1,0:T(8,128)(2,1)S(1)} collective-permute-done((bf16[160,1280]{1,0:T(8,128)(2,1)}, bf16[160,1280]{1,0:T(8,128)(2,1)S(1)}, u32[]{:S(2)}, u32[]{:S(2)}) %collective-permute-start.4) | collective-permute-done | bytes 409632 | tf_op jit(solution)/shard_map/ppermute | solution.py:256
  48.0 5.2 %collective-permute-start.5 = (bf16[160,1280]{1,0:T(8,128)(2,1)S(1)}, bf16[160,1280]{1,0:T(8,128)(2,1)}, u32[]{:S(2)}, u32[]{:S(2)}) collective-permute-start(bf16[160,1280]{1,0:T(8,128)(2,1)S(1)} %collective-permute-done.4.refs_2_), channel_id=1, source_target_pairs={{0,64},{1,449},{2,66},{3,451},{4,68},{5,453},{6,70},{7,455},{8,72}... | collective-permute-start | bytes 1228808 | tf_op jit(solution)/shard_map/ppermute | solution.py:256
  54.1 1.9 %collective-permute-start.8 = (bf16[5120,256]{1,0:T(8,128)(2,1)S(1)}, bf16[5120,256]{1,0:T(8,128)(2,1)}, u32[]{:S(2)}, u32[]{:S(2)}) collective-permute-start(bf16[5120,256]{1,0:T(8,128)(2,1)S(1)} %copy-done), channel_id=1, source_target_pairs={{0,1},{1,0},{2,3},{3,2},{4,5},{5,4},{6,7},{7,6},{8,9},{9,8},{10,11... | collective-permute-start | bytes 7864328 | tf_op jit(solution)/shard_map/ppermute | solution.py:245
  56.0 2.2 %collective-permute-done.5.refs_3_ = bf16[160,1280]{1,0:T(8,128)(2,1)} collective-permute-done((bf16[160,1280]{1,0:T(8,128)(2,1)S(1)}, bf16[160,1280]{1,0:T(8,128)(2,1)}, u32[]{:S(2)}, u32[]{:S(2)}) %collective-permute-start.5) | collective-permute-done | bytes 409632 | tf_op jit(solution)/shard_map/ppermute | solution.py:256
  60.3 2.3 %shard_map.113 = bf16[8,80,128]{2,1,0:T(8,128)(2,1)S(1)} custom-call(s32[1,2,4]{2,1,0:T(2,128)S(1)} %bitcast.10, bf16[1024,256]{1,0:T(8,128)(2,1)S(1)} %bitcast.6), custom_call_target="tpu_custom_call" | custom-call | flops 536870912 | bytes 1048576 | tf_op jit(solution)/shard_map/pallas_call | solution.py:312
  62.6 14.6 %all_to_all.21.heads_ref = bf16[8,80,128]{2,1,0:T(8,128)(2,1)S(1)} all-to-all(bf16[8,80,128]{2,1,0:T(8,128)(2,1)S(1)} %shard_map.113), channel_id=1, replica_groups={{0,2,4,6,8,10,12,14},{1,3,5,7,9,11,13,15},{16,18,20,22,24,26,28,30},{17..., dimensions={0} | all-to-all | bytes 327680 | tf_op jit(solution)/shard_map/all_to_all | solution.py:320
  79.1 1.8 %shard_map.114.own_ref = f32[128,1280]{1,0:T(8,128)S(1)} custom-call(bf16[8,80,128]{2,1,0:T(8,128)(2,1)S(1)} %all_to_all.21.heads_ref, bf16[1,64,1280]{2,1,0:T(8,128)(2,1)S(1)} %copy-done.3, bf16[160,1280]{1,0:T(8,128)(2,1)S(1)} %pad_maximum_fusion.refs_0_, bf16[160,1280]{1,0:T(8,128)(2,1)} %collective-permute-done.3.refs_1_, ...), custom_call_target="tpu_custom_call" | custom-call | flops 268435456 | bytes 3145728 | tf_op jit(solution)/shard_map/pallas_call | solution.py:328
  80.9 7.2 %collective-permute-start.7 = (f32[128,1280]{1,0:T(8,128)S(1)}, f32[128,1280]{1,0:T(8,128)S(1)}, u32[]{:S(2)}, u32[]{:S(2)}) collective-permute-start(f32[128,1280]{1,0:T(8,128)S(1)} %shard_map.114.own_ref), channel_id=1, source_target_pairs={{0,1},{1,0},{2,3},{3,2},{4,5},{5,4},{6,7},{7,6},{8,9},{9,8},{10,11... | collective-permute-start | bytes 1966088 | tf_op jit(solution)/shard_map/ppermute | solution.py:245
  90.8 1.9 %collective-permute-start.9 = (bf16[128,1280]{1,0:T(8,128)(2,1)S(1)}, bf16[128,1280]{1,0:T(8,128)(2,1)S(1)}, u32[]{:S(2)}, u32[]{:S(2)}) collective-permute-start(bf16[128,1280]{1,0:T(8,128)(2,1)S(1)} %get-tuple-element.8.refs_0_), channel_id=1, source_target_pairs={{0,2},{1,15},{2,4},{3,1},{4,6},{5,3},{6,8},{7,5},{8,10},{9,7},{10,... | collective-permute-start | bytes 983048 | tf_op jit(solution)/shard_map/ppermute | solution.py:256
  92.7 6.2 %collective-permute-done.9.refs_1_ = bf16[128,1280]{1,0:T(8,128)(2,1)S(1)} collective-permute-done((bf16[128,1280]{1,0:T(8,128)(2,1)S(1)}, bf16[128,1280]{1,0:T(8,128)(2,1)S(1)}, u32[]{:S(2)}, u32[]{:S(2)}) %collective-permute-start.9) | collective-permute-done | bytes 327712 | tf_op jit(solution)/shard_map/ppermute | solution.py:256
  98.9 2.8 %collective-permute-start.10 = (bf16[128,1280]{1,0:T(8,128)(2,1)S(1)}, bf16[128,1280]{1,0:T(8,128)(2,1)S(1)}, u32[]{:S(2)}, u32[]{:S(2)}) collective-permute-start(bf16[128,1280]{1,0:T(8,128)(2,1)S(1)} %collective-permute-done.9.refs_1_), channel_id=1, source_target_pairs={{0,2},{1,15},{2,4},{3,1},{4,6},{5,3},{6,8},{7,5},{8,10},{9,7},{10,... | collective-permute-start | bytes 983048 | tf_op jit(solution)/shard_map/ppermute | solution.py:256
  101.8 5.0 %collective-permute-done.10.refs_2_ = bf16[128,1280]{1,0:T(8,128)(2,1)S(1)} collective-permute-done((bf16[128,1280]{1,0:T(8,128)(2,1)S(1)}, bf16[128,1280]{1,0:T(8,128)(2,1)S(1)}, u32[]{:S(2)}, u32[]{:S(2)}) %collective-permute-start.10) | collective-permute-done | bytes 327712 | tf_op jit(solution)/shard_map/ppermute | solution.py:256
  106.7 4.0 %collective-permute-start.11 = (bf16[128,1280]{1,0:T(8,128)(2,1)S(1)}, bf16[128,1280]{1,0:T(8,128)(2,1)S(1)}, u32[]{:S(2)}, u32[]{:S(2)}) collective-permute-start(bf16[128,1280]{1,0:T(8,128)(2,1)S(1)} %collective-permute-done.10.refs_2_), channel_id=1, source_target_pairs={{0,2},{1,15},{2,4},{3,1},{4,6},{5,3},{6,8},{7,5},{8,10},{9,7},{10,... | collective-permute-start | bytes 983048 | tf_op jit(solution)/shard_map/ppermute | solution.py:256
  110.8 4.0 %collective-permute-done.11.refs_3_ = bf16[128,1280]{1,0:T(8,128)(2,1)S(1)} collective-permute-done((bf16[128,1280]{1,0:T(8,128)(2,1)S(1)}, bf16[128,1280]{1,0:T(8,128)(2,1)S(1)}, u32[]{:S(2)}, u32[]{:S(2)}) %collective-permute-start.11) | collective-permute-done | bytes 327712 | tf_op jit(solution)/shard_map/ppermute | solution.py:256
  115.5 2.8 %shard_map.116 = f32[16,128]{1,0:T(8,128)S(1)} custom-call(s32[1,2,4]{2,1,0:T(2,128)S(1)} %bitcast.11, s32[1,4]{1,0:T(1,128)S(1)} %copy-done.8, bf16[5120,256]{1,0:T(8,128)(2,1)S(1)} %copy-done, bf16[5120,256]{1,0:T(8,128)(2,1)} %collective-permute-done.8.wb_ref, bf16[128,1280]{1,0:T(8,128)(2,1)S(1)} %get-tuple-element.8.refs_0_, ...), custom_call_target="tpu_custom_call" | custom-call | flops 536870912 | bytes 7340032 | tf_op jit(solution)/shard_map/pallas_call | solution.py:349
  118.3 25.8 %all_to_all.22 = f32[16,1,128]{2,1,0:T(1,128)S(1)} all-to-all(f32[16,1,128]{2,1,0:T(1,128)S(1)} %bitcast.7), channel_id=1, replica_groups=mesh['rows'=32,'seq'=16] {'seq'}, dimensions={0} | all-to-all | bytes 16384 | tf_op jit(solution)/shard_map/all_to_all | solution.py:357
  (32 shorter events, 10.7 us)
Async XLA Ops:
  0.6 53.4 %copy-start = (bf16[5120,256]{1,0:T(8,128)(2,1)S(1)}, bf16[5120,256]{1,0:T(8,128)(2,1)}, u32[]{:S(2)}) copy-start(bf16[5120,256]{1,0:T(8,128)(2,1)} %wa_ref.1) | copy-start | bytes 7864324
  0.6 11.1 %collective-permute-start.1 = (bf16[40,1280]{1,0:T(8,128)(2,1)}, bf16[40,1280]{1,0:T(8,128)(2,1)S(1)}, u32[]{:S(2)}, u32[]{:S(2)}) collective-permute-start(bf16[40,1280]{1,0:T(8,128)(2,1)} %param.15), channel_id=1, source_target_pairs={{0,32},{16,48},{32,0},{48,16},{64,96},{80,112},{96,64},{112,80},{1... | collective-permute-start | bytes 307208 | tf_op jit(solution)/shard_map/ppermute | solution.py:264
  6.4 5.6 %collective-permute-start = (bf16[40,1280]{1,0:T(8,128)(2,1)}, bf16[40,1280]{1,0:T(8,128)(2,1)S(1)}, u32[]{:S(2)}, u32[]{:S(2)}) collective-permute-start(bf16[40,1280]{1,0:T(8,128)(2,1)} %param.15), channel_id=1, source_target_pairs={{0,48},{16,0},{32,16},{48,32},{64,112},{80,64},{96,80},{112,96},{1... | collective-permute-start | bytes 307208 | tf_op jit(solution)/shard_map/ppermute | solution.py:264
  9.2 7.6 %collective-permute-start.2 = (bf16[40,1280]{1,0:T(8,128)(2,1)}, bf16[40,1280]{1,0:T(8,128)(2,1)S(1)}, u32[]{:S(2)}, u32[]{:S(2)}) collective-permute-start(bf16[40,1280]{1,0:T(8,128)(2,1)} %param.15), channel_id=1, source_target_pairs={{0,16},{16,32},{32,48},{48,0},{64,80},{80,96},{96,112},{112,64},{1... | collective-permute-start | bytes 307208 | tf_op jit(solution)/shard_map/ppermute | solution.py:264
  17.7 20.9 %collective-permute-start.3 = (bf16[160,1280]{1,0:T(8,128)(2,1)S(1)}, bf16[160,1280]{1,0:T(8,128)(2,1)}, u32[]{:S(2)}, u32[]{:S(2)}) collective-permute-start(bf16[160,1280]{1,0:T(8,128)(2,1)S(1)} %pad_maximum_fusion.refs_0_), channel_id=1, source_target_pairs={{0,64},{1,449},{2,66},{3,451},{4,68},{5,453},{6,70},{7,455},{8,72}... | collective-permute-start | bytes 1228808 | tf_op jit(solution)/shard_map/ppermute | solution.py:256
  31.4 28.1 %all-to-all-start = ((bf16[16,64,256]{2,1,0:T(8,128)(2,1)}), bf16[16,64,256]{2,1,0:T(8,128)(2,1)S(1)}, u32[]{:S(2)}, u32[]{:S(2)}) async-start(bf16[16,64,256]{2,1,0:T(8,128)(2,1)} %shard_map.112), calls=%async_computation | async-start | bytes 1048576 | tf_op jit(solution)/shard_map/all_to_all | solution.py:310
  38.7 9.4 %collective-permute-start.4 = (bf16[160,1280]{1,0:T(8,128)(2,1)}, bf16[160,1280]{1,0:T(8,128)(2,1)S(1)}, u32[]{:S(2)}, u32[]{:S(2)}) collective-permute-start(bf16[160,1280]{1,0:T(8,128)(2,1)} %collective-permute-done.3.refs_1_), channel_id=1, source_target_pairs={{0,64},{1,449},{2,66},{3,451},{4,68},{5,453},{6,70},{7,455},{8,72}... | collective-permute-start | bytes 1228808 | tf_op jit(solution)/shard_map/ppermute | solution.py:256
  48.0 10.1 %collective-permute-start.5 = (bf16[160,1280]{1,0:T(8,128)(2,1)S(1)}, bf16[160,1280]{1,0:T(8,128)(2,1)}, u32[]{:S(2)}, u32[]{:S(2)}) collective-permute-start(bf16[160,1280]{1,0:T(8,128)(2,1)S(1)} %collective-permute-done.4.refs_2_), channel_id=1, source_target_pairs={{0,64},{1,449},{2,66},{3,451},{4,68},{5,453},{6,70},{7,455},{8,72}... | collective-permute-start | bytes 1228808 | tf_op jit(solution)/shard_map/ppermute | solution.py:256
  53.3 0.8 copy-start.1
  54.1 61.4 %collective-permute-start.8 = (bf16[5120,256]{1,0:T(8,128)(2,1)S(1)}, bf16[5120,256]{1,0:T(8,128)(2,1)}, u32[]{:S(2)}, u32[]{:S(2)}) collective-permute-start(bf16[5120,256]{1,0:T(8,128)(2,1)S(1)} %copy-done), channel_id=1, source_target_pairs={{0,1},{1,0},{2,3},{3,2},{4,5},{5,4},{6,7},{7,6},{8,9},{9,8},{10,11... | collective-permute-start | bytes 7864328 | tf_op jit(solution)/shard_map/ppermute | solution.py:245
  58.1 19.1 %collective-permute-start.6 = (bf16[160,1280]{1,0:T(8,128)(2,1)}, bf16[160,1280]{1,0:T(8,128)(2,1)}, u32[]{:S(2)}, u32[]{:S(2)}) collective-permute-start(bf16[160,1280]{1,0:T(8,128)(2,1)} %collective-permute-done.5.refs_3_), channel_id=1, source_target_pairs={{0,64},{2,66},{4,68},{6,70},{8,72},{10,74},{12,76},{14,78},{16,80}... | collective-permute-start | bytes 1228808 | tf_op jit(solution)/shard_map/ppermute | solution.py:256
  59.6 0.7 copy-start.4
  60.2 29.5 %copy-start.6 = (f32[1280]{0:T(1024)S(1)}, f32[1280]{0:T(1024)}, u32[]{:S(2)}) copy-start(f32[1280]{0:T(1024)} %gain_ref.1) | copy-start | bytes 15364
  60.3 29.5 %copy-start.7 = (f32[1280]{0:T(1024)S(1)}, f32[1280]{0:T(1024)}, u32[]{:S(2)}) copy-start(f32[1280]{0:T(1024)} %bias_ref.1) | copy-start | bytes 15364
  62.6 52.9 %copy-start.5 = (s32[1,4,2]{1,2,0:T(2,128)S(1)}, s32[1,4,2]{1,2,0:T(2,128)}, u32[]{:S(2)}) copy-start(s32[1,4,2]{1,2,0:T(2,128)} %param.13) | copy-start | bytes 100
  62.6 52.9 %copy-start.8 = (s32[1,4]{1,0:T(1,128)S(1)}, s32[1,4]{1,0:T(1,128)}, u32[]{:S(2)}) copy-start(s32[1,4]{1,0:T(1,128)} %owner_ref.3) | copy-start | bytes 52
  77.2 1.0 copy-start.2
  78.2 0.9 copy-start.3
  80.9 8.9 %collective-permute-start.7 = (f32[128,1280]{1,0:T(8,128)S(1)}, f32[128,1280]{1,0:T(8,128)S(1)}, u32[]{:S(2)}, u32[]{:S(2)}) collective-permute-start(f32[128,1280]{1,0:T(8,128)S(1)} %shard_map.114.own_ref), channel_id=1, source_target_pairs={{0,1},{1,0},{2,3},{3,2},{4,5},{5,4},{6,7},{7,6},{8,9},{9,8},{10,11... | collective-permute-start | bytes 1966088 | tf_op jit(solution)/shard_map/ppermute | solution.py:245
  90.8 8.1 %collective-permute-start.9 = (bf16[128,1280]{1,0:T(8,128)(2,1)S(1)}, bf16[128,1280]{1,0:T(8,128)(2,1)S(1)}, u32[]{:S(2)}, u32[]{:S(2)}) collective-permute-start(bf16[128,1280]{1,0:T(8,128)(2,1)S(1)} %get-tuple-element.8.refs_0_), channel_id=1, source_target_pairs={{0,2},{1,15},{2,4},{3,1},{4,6},{5,3},{6,8},{7,5},{8,10},{9,7},{10,... | collective-permute-start | bytes 983048 | tf_op jit(solution)/shard_map/ppermute | solution.py:256
  98.9 7.8 %collective-permute-start.10 = (bf16[128,1280]{1,0:T(8,128)(2,1)S(1)}, bf16[128,1280]{1,0:T(8,128)(2,1)S(1)}, u32[]{:S(2)}, u32[]{:S(2)}) collective-permute-start(bf16[128,1280]{1,0:T(8,128)(2,1)S(1)} %collective-permute-done.9.refs_1_), channel_id=1, source_target_pairs={{0,2},{1,15},{2,4},{3,1},{4,6},{5,3},{6,8},{7,5},{8,10},{9,7},{10,... | collective-permute-start | bytes 983048 | tf_op jit(solution)/shard_map/ppermute | solution.py:256
  106.7 8.0 %collective-permute-start.11 = (bf16[128,1280]{1,0:T(8,128)(2,1)S(1)}, bf16[128,1280]{1,0:T(8,128)(2,1)S(1)}, u32[]{:S(2)}, u32[]{:S(2)}) collective-permute-start(bf16[128,1280]{1,0:T(8,128)(2,1)S(1)} %collective-permute-done.10.refs_2_), channel_id=1, source_target_pairs={{0,2},{1,15},{2,4},{3,1},{4,6},{5,3},{6,8},{7,5},{8,10},{9,7},{10,... | collective-permute-start | bytes 983048 | tf_op jit(solution)/shard_map/ppermute | solution.py:256
  114.8 0.7 collective-permute-start.12
